TPU v7x, 128 devices: a whole 4x4x4 slice. The times are simulated.
128 devices in a mesh: grp: 2 (over z_hi), wid: 8 (over y, core), hid: 8 (over z_lo, x).
Axes of the slice: x: 4, y: 4, z: 4 (z_hi: 2, z_lo: 2; z = z_hi * 2 + z_lo), core: 2. Of those that a mesh axis runs over, the one named last changes fastest.
Arguments:
- student_in: bfloat16 [1024, 4096], P('wid'), may hold values from -6 to 6
- norm_gain: float32 [4096], replicated, may hold values from 0.1 to 1.9
- gate_weight: bfloat16 [4096, 7168], P(None, ('grp', 'hid')), may hold values from -0.09375 to 0.09375
- up_weight: bfloat16 [4096, 7168], P(None, ('grp', 'hid')), may hold values from -0.09375 to 0.09375
- down_weight: bfloat16 [7168, 4096], P(('grp', 'hid')), may hold values from -0.0625 to 0.0625
- projection: bfloat16 [4096, 8, 1024], P(None, None, ('grp', 'hid')), may hold values from -0.09375 to 0.09375
- teacher_in: bfloat16 [1024, 8192], P(None, 'wid'), may hold values from -6 to 6
- teacher_gate: bfloat16 [8192, 14336], P('wid', ('grp', 'hid')), may hold values from -0.0625 to 0.0625
- teacher_up: bfloat16 [8192, 14336], P('wid', ('grp', 'hid')), may hold values from -0.0625 to 0.0625
- teacher_down: bfloat16 [14336, 8192], P(('grp', 'hid'), 'wid'), may hold values from -0.046875 to 0.046875
Outputs:
- grad_gate: bfloat16 [4096, 7168], P('wid', ('grp', 'hid'))
- grad_up: bfloat16 [4096, 7168], P('wid', ('grp', 'hid'))
- grad_down: bfloat16 [7168, 4096], P(('grp', 'hid'), 'wid')
- grad_proj: bfloat16 [4096, 8, 1024], P('wid', None, ('grp', 'hid'))
- input_grad: float32 [1024, 4096], P('wid', ('grp', 'hid'))
All inputs are finite; a program needn't handle non-finite values.
Results may differ from a plain program's by a relative error of at most 0.02.
Values may be sent and summed in bfloat16 or wider, within the bound.
A program may use at most 128 MiB of HBM per device.

v0:
```python
import math

import jax
import jax.numpy as jnp
from jax import lax
from jax.sharding import Mesh
from jax.sharding import PartitionSpec as P

WID = ("wid_0", "wid_1")
GRP_HID = ("grp", "hid_0", "hid_1")


def split_up(array, dim, peers):
    shape = array.shape
    blocks = array.reshape(*shape[:dim], peers, shape[dim] // peers, *shape[dim + 1 :])
    return jnp.moveaxis(blocks, dim, 0)


def one_scatter(arrays, axis, dims):
    peers = lax.axis_size(axis)
    blocks = [split_up(a, dim, peers) for a, dim in zip(arrays, dims)]
    lines = jnp.concatenate([b.reshape(peers, -1) for b in blocks], axis=1)
    rows = max(16, -(-lines.shape[1] // 1024) * 8)
    lines = jnp.pad(lines, ((0, 0), (0, rows * 128 - lines.shape[1]))).reshape(-1, 128)
    vector, at, done = (lax.psum_scatter(lines, axis, tiled=True).reshape(-1), 0, [])
    for b in blocks:
        part = b[0]
        done.append(vector[at : at + part.size].reshape(part.shape))
        at += part.size
    return tuple(done)


def from_everyone(array, axis):
    peers = lax.axis_size(axis)
    return lax.all_to_all(
        jnp.broadcast_to(array[None], (peers, *array.shape)), axis, 0, 0, tiled=True
    )


def joined_along(blocks, dim):
    blocks = jnp.moveaxis(blocks, 0, dim)
    shape = blocks.shape
    return blocks.reshape(*shape[:dim], shape[dim] * shape[dim + 1], *shape[dim + 2 :])


def whole_of(array, axes, dim):
    far, near = axes
    blocks = from_everyone(from_everyone(array, far), near)
    return joined_along(blocks.swapaxes(0, 1).reshape(-1, *array.shape), dim)


def sent_and_summed(array, axis, dim):
    blocks = split_up(array, dim, lax.axis_size(axis))
    arrived = lax.all_to_all(blocks, axis, split_axis=0, concat_axis=0, tiled=True)
    return arrived.astype(jnp.float32).sum(axis=0)


def summed_rows(array, axes, dim):
    far, near = axes
    blocks = split_up(array, dim, lax.axis_size(far))
    nearer = sent_and_summed(blocks, near, dim + 1)
    arrived = lax.all_to_all(
        nearer.astype(jnp.bfloat16), far, split_axis=0, concat_axis=0, tiled=True
    )
    return arrived.astype(jnp.float32).sum(axis=0)


def rows_for(lines, peers):
    spare = -len(lines) % peers
    return jnp.pad(lines, [(0, spare)] + [(0, 0)] * (lines.ndim - 1))


def total_of(array, axes):
    lines = array.reshape(-1, array.shape[-1])
    own = summed_rows(rows_for(lines, lax.axis_size(axes[0]) * lax.axis_size(axes[1])), axes, 0)
    whole = whole_of(own.astype(jnp.bfloat16), axes, 0)
    return whole[: len(lines)].reshape(array.shape).astype(jnp.float32)


def of_everyone(array, axis):
    everything = from_everyone(array, axis)
    return jnp.sum(everything, axis=0)


def in_one_piece(arrays, axis, dim, along):
    ends, at = ([], 0)
    for a in arrays[:-1]:
        at += a.shape[along]
        ends.append(at)
    both = jnp.concatenate(arrays, axis=along)
    return tuple(jnp.split(lax.all_gather(both, axis, axis=dim, tiled=True), ends, axis=along))


def shards(
    student_in,
    norm_gain,
    gate_weight,
    up_weight,
    down_weight,
    projection,
    teacher_in,
    teacher_gate,
    teacher_up,
    teacher_down,
):
    f32 = jnp.float32
    bf16 = jnp.bfloat16
    gate_part = jnp.dot(teacher_in, teacher_gate, preferred_element_type=f32)
    up_part = jnp.dot(teacher_in, teacher_up, preferred_element_type=f32)
    gate_rows, up_rows = tuple(
        (
            part.astype(jnp.float32)
            for part in one_scatter(
                (gate_part.astype(jnp.bfloat16), up_part.astype(jnp.bfloat16)), WID, (0, 0)
            )
        )
    )
    teacher_hidden = (gate_rows * jax.nn.sigmoid(gate_rows) * up_rows).astype(bf16)
    feature_part = jnp.dot(
        whole_of(teacher_hidden, ("wid_0", "wid_1"), 0), teacher_down, preferred_element_type=f32
    )
    target_cols = (
        lax.psum_scatter(
            feature_part.astype(jnp.bfloat16), GRP_HID, scatter_dimension=1, tiled=True
        )
        .astype(jnp.float32)
        .astype(bf16)
    )
    target = lax.all_to_all(target_cols, WID, split_axis=0, concat_axis=1, tiled=True)
    tokens_dev = student_in.shape[0]
    width = student_in.shape[1]
    total_tokens = tokens_dev * lax.axis_size(WID)
    inputs = student_in.astype(f32)
    inverse_rms = lax.rsqrt(jnp.mean(inputs * inputs, axis=-1, keepdims=True) + 1e-05)
    normed = (inputs * inverse_rms * norm_gain).astype(bf16)
    gate_sum = jnp.dot(normed, gate_weight, preferred_element_type=f32)
    up_sum = jnp.dot(normed, up_weight, preferred_element_type=f32)
    sigma = jax.nn.sigmoid(gate_sum)
    hidden = (gate_sum * sigma * up_sum).astype(bf16)
    branch = total_of(
        jnp.dot(hidden, down_weight, preferred_element_type=f32).astype(jnp.bfloat16),
        ("grp", ("hid_0", "hid_1")),
    )
    summed = (inputs + branch).astype(bf16)
    proj_local = projection.reshape(width, -1)
    features = jnp.dot(summed, proj_local, preferred_element_type=f32)
    feature_error = ((features - target.astype(f32)) / math.sqrt(total_tokens)).astype(bf16)
    feature_grad = total_of(
        jnp.dot(feature_error, proj_local.T, preferred_element_type=f32).astype(jnp.bfloat16),
        ("grp", ("hid_0", "hid_1")),
    )
    branch_grad = feature_grad.astype(bf16)
    hidden_grad = jnp.dot(branch_grad, down_weight.T, preferred_element_type=f32)
    gate_grad = (hidden_grad * up_sum * sigma * (1.0 + gate_sum * (1.0 - sigma))).astype(bf16)
    up_grad = (hidden_grad * gate_sum * sigma).astype(bf16)
    normed_grad = jnp.dot(gate_grad, gate_weight.T, preferred_element_type=f32) + jnp.dot(
        up_grad, up_weight.T, preferred_element_type=f32
    )
    share_cols = width // lax.axis_size(GRP_HID)
    offset = lax.axis_index(GRP_HID) * share_cols
    normed_share = sent_and_summed(normed_grad.astype(jnp.bfloat16), GRP_HID, 1)
    input_share = lax.dynamic_slice_in_dim(inputs, offset, share_cols, 1)
    gain_share = lax.dynamic_slice_in_dim(norm_gain, offset, share_cols, 0)
    scaled = normed_share * gain_share
    moment = of_everyone(jnp.sum(scaled * input_share, axis=-1, keepdims=True), GRP_HID) / width
    grad_share = lax.dynamic_slice_in_dim(feature_grad, offset, share_cols, 1)
    input_grad = grad_share + inverse_rms * (
        scaled - input_share * inverse_rms * inverse_rms * moment
    )
    paired_grad = jnp.concatenate([gate_grad, up_grad], axis=1)
    summed_cols, branch_cols = (
        lax.all_to_all(summed, WID, split_axis=1, concat_axis=0, tiled=True),
        lax.all_to_all(branch_grad, WID, split_axis=1, concat_axis=0, tiled=True),
    )
    hidden_all, error_all = in_one_piece((hidden, feature_error), WID, 0, 1)
    weight_grad = lax.psum_scatter(
        jnp.dot(normed.T, paired_grad, preferred_element_type=f32).astype(jnp.bfloat16),
        WID,
        scatter_dimension=0,
        tiled=True,
    ).astype(jnp.float32)
    hidden_cols = gate_grad.shape[1]
    grad_gate = weight_grad[:, :hidden_cols].astype(bf16)
    grad_up = weight_grad[:, hidden_cols:].astype(bf16)
    grad_down = jnp.dot(hidden_all.T, branch_cols, preferred_element_type=f32).astype(bf16)
    grad_proj = jnp.dot(summed_cols.T, error_all, preferred_element_type=f32).astype(bf16)
    grad_proj = grad_proj.reshape(summed_cols.shape[1], lax.axis_size(WID), -1)
    return (grad_gate, grad_up, grad_down, grad_proj, input_grad)


def solution(mesh):
    split = Mesh(
        mesh.devices.reshape(mesh.shape["grp"], 4, 2, 2, 4),
        ("grp", "wid_0", "wid_1", "hid_0", "hid_1"),
    )
    in_specs = (
        P(WID, None),
        P(),
        P(None, GRP_HID),
        P(None, GRP_HID),
        P(GRP_HID, None),
        P(None, None, GRP_HID),
        P(None, WID),
        P(WID, GRP_HID),
        P(WID, GRP_HID),
        P(GRP_HID, WID),
    )
    out_specs = (
        P(WID, GRP_HID),
        P(WID, GRP_HID),
        P(GRP_HID, WID),
        P(WID, None, GRP_HID),
        P(WID, GRP_HID),
    )
    return jax.shard_map(
        shards, mesh=split, in_specs=in_specs, out_specs=out_specs, check_vma=False
    )
```

profile of v0, /device:TPU:1, one launch (start us, length us, event | category | flops | bytes accessed | tf_op | source)
XLA Modules:
  0.0 364.6 jit_solution(1658961827756413029)
XLA Ops:
  7.2 1.5 copy-done
  8.8 5.1 %convolution_convert_fusion.5 = bf16[1024,896]{1,0:T(8,128)(2,1)} fusion(bf16[1024,1024]{1,0:T(8,128)(2,1)S(1)} %copy-done, bf16[1024,896]{1,0:T(8,128)(2,1)} %param.17), kind=kOutput, calls=%fused_computation.13 | convolution fusion | flops 1879965696 | bytes 5767168 | tf_op jit(solution)/shard_map/dot_general | solution.py:108
  13.8 3.6 reshape_reshape.20
  17.4 5.1 %convolution_convert_fusion.4 = bf16[1024,896]{1,0:T(8,128)(2,1)} fusion(bf16[1024,1024]{1,0:T(8,128)(2,1)S(1)} %copy-done, bf16[1024,896]{1,0:T(8,128)(2,1)} %param.18), kind=kOutput, calls=%fused_computation.12 | convolution fusion | flops 1879965696 | bytes 5767168 | tf_op jit(solution)/shard_map/dot_general | solution.py:109
  22.5 3.7 %reshape_reshape.21 = bf16[8,114688]{1,0:T(8,128)(2,1)} reshape(bf16[1024,896]{1,0:T(8,128)(2,1)} %convolution_convert_fusion.4) | data formatting | bytes 3670016 | tf_op jit(solution)/shard_map/reshape;reshape | solution.py:22
  26.2 8.3 %pad_maximum_fusion = bf16[8,229376]{1,0:T(8,128)(2,1)} fusion(bf16[8,114688]{1,0:T(8,128)(2,1)} %reshape_reshape.21, bf16[8,114688]{1,0:T(8,128)(2,1)S(1)} %copy-done.3), kind=kLoop, calls=%fused_computation.5 | loop fusion | flops 7340032 | bytes 7340032 | tf_op jit(solution)/shard_map/concatenate | solution.py:22
  34.5 5.5 %reshape.88 = bf16[14336,128]{1,0:T(8,128)(2,1)} reshape(bf16[8,229376]{1,0:T(8,128)(2,1)} %pad_maximum_fusion) | data formatting | bytes 7340032 | tf_op jit(solution)/shard_map/reshape | solution.py:24
  40.1 37.3 %reduce-scatter.4.cloned.1.call-done = bf16[1792,128]{1,0:T(8,128)(2,1)} async-done(((bf16[14336,128]{1,0:T(8,128)(2,1)}), bf16[1792,128]{1,0:T(8,128)(2,1)}) %reduce-scatter.4.cloned.1.call-update) | async-done | bytes 458768 | tf_op jit(solution)/shard_map/reduce_scatter | solution.py:25
  77.4 1.1 slice_convert_fusion.1
  78.9 1.0 broadcast_in_dim.16
  79.9 4.9 %all-to-all-start.4 = ((bf16[4,128,896]{2,1,0:T(8,128)(2,1)}), bf16[4,128,896]{2,1,0:T(8,128)(2,1)S(1)}, u32[]{:S(2)}, u32[]{:S(2)}) async-start(bf16[4,128,896]{2,1,0:T(8,128)(2,1)} %broadcast_in_dim.16), calls=%async_computation.5 | async-start | bytes 1835008 | tf_op jit(solution)/shard_map/all_to_all | solution.py:35
  85.1 11.0 %all-to-all-done.4 = bf16[4,128,896]{2,1,0:T(8,128)(2,1)S(1)} async-done(((bf16[4,128,896]{2,1,0:T(8,128)(2,1)}), bf16[4,128,896]{2,1,0:T(8,128)(2,1)S(1)}, u32[]{:S(2)}, u32[]{:S(2)}) %all-to-all-start.4) | async-done | bytes 917536 | tf_op jit(solution)/shard_map/all_to_all | solution.py:35
  96.3 8.3 %all_to_all.111 = bf16[2,4,128,896]{3,2,1,0:T(8,128)(2,1)S(1)} all-to-all(bf16[2,4,128,896]{3,2,1,0:T(8,128)(2,1)S(1)} %broadcast_in_dim.17), channel_id=1, replica_groups=mesh['grp'=2,'wid_0'=4,'wid_1'=2,'hid_0'=2,'hid_1'=4] {'wid_1'}, dimensions={0} | all-to-all | bytes 3670016 | tf_op jit(solution)/shard_map/all_to_all | solution.py:35
  104.8 1.3 copy-done.11
  106.1 3.7 %convolution_convert_fusion.3 = bf16[1024,1024]{0,1:T(8,128)(2,1)} fusion(bf16[1024,896]{1,0:T(8,128)(2,1)S(1)} %bitcast.83, bf16[896,1024]{1,0:T(8,128)(2,1)S(1)} %copy-done.11), kind=kOutput, calls=%fused_computation.11 | convolution fusion | flops 1880096768 | bytes 5767168 | tf_op jit(solution)/shard_map/dot_general | solution.py:119
  109.9 0.7 copy-done.9
  110.5 3.4 fusion.11
  113.9 1.9 multiply_convert_fusion.4
  116.1 0.8 convolution_convert_fusion.2
  116.9 23.1 %all_to_all.112 = bf16[8,2,8,4096]{3,2,1,0:T(8,128)(2,1)S(1)} all-to-all(bf16[8,2,8,4096]{3,2,1,0:T(8,128)(2,1)S(1)} %bitcast.78), channel_id=1, replica_groups=mesh['grp'=2,'wid_0'=4,'wid_1'=2,'hid_0'=2,'hid_1'=4] {'hid_0','hid_1'}, dimensions={0} | all-to-all | bytes 2097152 | tf_op jit(solution)/shard_map/all_to_all | solution.py:54
  140.2 8.4 %all_to_all.113 = bf16[2,8,4096]{2,1,0:T(8,128)(2,1)S(1)} all-to-all(bf16[2,8,4096]{2,1,0:T(8,128)(2,1)S(1)} %reduce_sum.85), channel_id=1, replica_groups=mesh['grp'=2,'wid_0'=4,'wid_1'=2,'hid_0'=2,'hid_1'=4] {'grp'}, dimensions={0} | all-to-all | bytes 262144 | tf_op jit(solution)/shard_map/all_to_all | solution.py:62
  148.6 7.3 %all_to_all.114 = bf16[2,8,4096]{2,1,0:T(8,128)(2,1)S(1)} all-to-all(bf16[2,8,4096]{2,1,0:T(8,128)(2,1)S(1)} %broadcast_in_dim.14), channel_id=1, replica_groups=mesh['grp'=2,'wid_0'=4,'wid_1'=2,'hid_0'=2,'hid_1'=4] {'grp'}, dimensions={0} | all-to-all | bytes 262144 | tf_op jit(solution)/shard_map/all_to_all | solution.py:35
  155.9 1.1 broadcast_in_dim.15
  157.0 3.6 all-to-all-start.3
  160.7 15.1 %all-to-all-done.3 = bf16[8,2,8,4096]{3,2,1,0:T(8,128)(2,1)S(1)} async-done(((bf16[8,2,8,4096]{3,2,1,0:T(8,128)(2,1)}), bf16[8,2,8,4096]{3,2,1,0:T(8,128)(2,1)S(1)}, u32[]{:S(2)}, u32[]{:S(2)}) %all-to-all-start.3) | async-done | bytes 1048608 | tf_op jit(solution)/shard_map/all_to_all | solution.py:35
  175.8 1.5 copy_convert_fusion
  177.3 13.6 %reduce-scatter.6.cloned.1.call-done = bf16[1024,64]{0,1:T(8,128)(2,1)} async-done(((bf16[1024,1024]{0,1:T(8,128)(2,1)}), bf16[1024,64]{0,1:T(8,128)(2,1)}) %reduce-scatter.6.cloned.1.call-update) | async-done | bytes 131088 | tf_op jit(solution)/shard_map/reduce_scatter | solution.py:123
  190.9 1.6 copy_bitcast_fusion.2
  192.5 6.6 %all-to-all-start.6 = ((bf16[8,128,64]{1,2,0:T(8,128)(2,1)}), bf16[8,128,64]{1,2,0:T(8,128)(2,1)S(1)}, u32[]{:S(2)}, u32[]{:S(2)}) async-start(bf16[8,128,64]{1,2,0:T(8,128)(2,1)} %copy_bitcast_fusion.2), calls=%async_computation.8 | async-start | bytes 262144 | tf_op jit(solution)/shard_map/all_to_all | solution.py:129
  199.1 1.8 fusion.1
  200.9 3.4 all-to-all-done.6
  204.5 3.7 %fusion.3 = bf16[128,512]{1,0:T(8,128)(2,1)S(1)} fusion(f32[128,512]{1,0:T(8,128)S(1)} %copy.60, bf16[128,4096]{1,0:T(8,128)(2,1)S(1)} %fusion.1, bf16[4096,512]{0,1:T(8,128)(2,1)} %bitcast.69), kind=kOutput, calls=%fused_computation.18 | convolution fusion | flops 537067520 | bytes 5636096 | tf_op jit(solution)/shard_map/dot_general | solution.py:146
  208.2 0.8 pad_maximum_fusion.1
  209.1 2.9 convolution_convert_fusion.1
  212.1 18.1 %all_to_all.115 = bf16[8,2,8,4096]{3,2,1,0:T(8,128)(2,1)S(1)} all-to-all(bf16[8,2,8,4096]{3,2,1,0:T(8,128)(2,1)S(1)} %bitcast.79), channel_id=1, replica_groups=mesh['grp'=2,'wid_0'=4,'wid_1'=2,'hid_0'=2,'hid_1'=4] {'hid_0','hid_1'}, dimensions={0} | all-to-all | bytes 2097152 | tf_op jit(solution)/shard_map/all_to_all | solution.py:54
  230.3 7.7 %all_to_all.116 = bf16[2,8,4096]{2,1,0:T(8,128)(2,1)S(1)} all-to-all(bf16[2,8,4096]{2,1,0:T(8,128)(2,1)S(1)} %reduce_sum.87), channel_id=1, replica_groups=mesh['grp'=2,'wid_0'=4,'wid_1'=2,'hid_0'=2,'hid_1'=4] {'grp'}, dimensions={0} | all-to-all | bytes 262144 | tf_op jit(solution)/shard_map/all_to_all | solution.py:62
  238.1 7.2 %all_to_all.117 = bf16[2,8,4096]{2,1,0:T(8,128)(2,1)S(1)} all-to-all(bf16[2,8,4096]{2,1,0:T(8,128)(2,1)S(1)} %broadcast_in_dim.18), channel_id=1, replica_groups=mesh['grp'=2,'wid_0'=4,'wid_1'=2,'hid_0'=2,'hid_1'=4] {'grp'}, dimensions={0} | all-to-all | bytes 262144 | tf_op jit(solution)/shard_map/all_to_all | solution.py:35
  245.5 14.4 %all_to_all.118 = bf16[8,2,8,4096]{3,2,1,0:T(8,128)(2,1)S(1)} all-to-all(bf16[8,2,8,4096]{3,2,1,0:T(8,128)(2,1)S(1)} %broadcast_in_dim.19), channel_id=1, replica_groups=mesh['grp'=2,'wid_0'=4,'wid_1'=2,'hid_0'=2,'hid_1'=4] {'hid_0','hid_1'}, dimensions={0} | all-to-all | bytes 2097152 | tf_op jit(solution)/shard_map/all_to_all | solution.py:35
  260.0 1.1 multiply_convert_fusion.3
  261.2 5.1 %convolution_convert_fusion = bf16[4096,896]{1,0:T(8,128)(2,1)} fusion(bf16[128,448]{0,1:T(8,128)(2,1)S(1)} %get-tuple-element.38, bf16[128,448]{0,1:T(8,128)(2,1)S(1)} %get-tuple-element.37, bf16[128,4096]{1,0:T(8,128)(2,1)S(1)} %copy-done.2, f32[4096]{0:T(1024)S(1)} %copy-done.9, f32[128]{0:T(128)S(1)} %add_rsqrt_fusion), kind=kOutput, calls=%fused_computation | convolution fusion | flops 945750016 | bytes 8634880 | tf_op jit(solution)/shard_map/dot_general | solution.py:177
  266.3 2.9 fusion.13
  269.5 0.8 fusion
  270.2 1.1 copy.78
  271.3 4.4 %all-to-all-start.13 = ((bf16[16,128,256]{2,1,0:T(8,128)(2,1)}), bf16[16,128,256]{2,1,0:T(8,128)(2,1)}, u32[]{:S(2)}, u32[]{:S(2)}) async-start(bf16[16,128,256]{2,1,0:T(8,128)(2,1)} %bitcast.77), calls=%async_computation.16 | async-start | bytes 2097152 | tf_op jit(solution)/shard_map/all_to_all | solution.py:54
  275.6 1.4 copy.65
  277.0 12.0 %all-to-all-done.13 = bf16[16,128,256]{2,1,0:T(8,128)(2,1)} async-done(((bf16[16,128,256]{2,1,0:T(8,128)(2,1)}), bf16[16,128,256]{2,1,0:T(8,128)(2,1)}, u32[]{:S(2)}, u32[]{:S(2)}) %all-to-all-start.13) | async-done | bytes 1048608 | tf_op jit(solution)/shard_map/all_to_all | solution.py:54
  289.0 9.0 %all-to-all-start.12 = ((bf16[128,8,512]{0,2,1:T(8,128)(2,1)}), bf16[128,8,512]{0,2,1:T(8,128)(2,1)S(1)}, u32[]{:S(2)}, u32[]{:S(2)}) async-start(bf16[128,8,512]{0,2,1:T(8,128)(2,1)} %bitcast.76), calls=%async_computation.15 | async-start | bytes 2097152 | tf_op jit(solution)/shard_map/all_to_all | solution.py:172
  298.0 1.5 convert_element_type.113
  299.6 1.4 convert_reduce_fusion
  301.0 1.0 multiply_reduce_fusion.1
  302.0 17.0 %all-to-all-done.12 = bf16[128,8,512]{0,2,1:T(8,128)(2,1)S(1)} async-done(((bf16[128,8,512]{0,2,1:T(8,128)(2,1)}), bf16[128,8,512]{0,2,1:T(8,128)(2,1)S(1)}, u32[]{:S(2)}, u32[]{:S(2)}) %all-to-all-start.12) | async-done | bytes 1048608 | tf_op jit(solution)/shard_map/all_to_all | solution.py:172
  319.0 0.6 broadcast_in_dim.20
  319.6 3.5 all-to-all-start.14
  323.5 1.3 copy.64
  324.8 4.6 %all-to-all-done.14 = f32[16,128,1]{1,2,0:T(1,128)S(1)} async-done(((f32[16,128,1]{1,2,0:T(1,128)}), f32[16,128,1]{1,2,0:T(1,128)S(1)}, u32[]{:S(2)}, u32[]{:S(2)}) %all-to-all-start.14) | async-done | bytes 8224 | tf_op jit(solution)/shard_map/all_to_all | solution.py:35
  329.4 5.5 %all-to-all-start.11 = ((bf16[128,8,512]{2,0,1:T(8,128)(2,1)}), bf16[128,8,512]{2,0,1:T(8,128)(2,1)S(1)}, u32[]{:S(2)}, u32[]{:S(2)}) async-start(bf16[128,8,512]{2,0,1:T(8,128)(2,1)} %copy.64), calls=%async_computation.14 | async-start | bytes 2097152 | tf_op jit(solution)/shard_map/all_to_all | solution.py:173
  334.9 1.4 copy.66
  336.3 1.7 multiply_add_fusion
  338.0 11.9 %all-to-all-done.11 = bf16[128,8,512]{2,0,1:T(8,128)(2,1)S(1)} async-done(((bf16[128,8,512]{2,0,1:T(8,128)(2,1)}), bf16[128,8,512]{2,0,1:T(8,128)(2,1)S(1)}, u32[]{:S(2)}, u32[]{:S(2)}) %all-to-all-start.11) | async-done | bytes 1048608 | tf_op jit(solution)/shard_map/all_to_all | solution.py:173
  349.9 2.8 convolution_convert_fusion.7
  352.8 1.9 convolution_convert_fusion.6
  354.7 1.5 fusion.12
  356.2 1.0 copy.69
  357.1 1.0 copy.68
  (61 shorter events, 3.1 us)
Async XLA Ops:
  7.2 1.6 copy-start
  7.2 70.2 %reduce-scatter.4.cloned.1.call-start = ((), (), s32[]{:S(2)}) async-start(), calls=%async_computation.18 | async-start | bytes 4128768 | tf_op jit(solution)/shard_map/reduce_scatter | solution.py:25
  22.5 3.7 %copy-start.3 = (bf16[8,114688]{1,0:T(8,128)(2,1)S(1)}, bf16[8,114688]{1,0:T(8,128)(2,1)}, u32[]{:S(2)}) copy-start(bf16[8,114688]{1,0:T(8,128)(2,1)} %reshape_reshape.20) | copy-start | bytes 5505028
  78.7 6.1 %copy-start.2 = (bf16[128,4096]{1,0:T(8,128)(2,1)S(1)}, bf16[128,4096]{1,0:T(8,128)(2,1)}, u32[]{:S(2)}) copy-start(bf16[128,4096]{1,0:T(8,128)(2,1)} %param.10) | copy-start | bytes 3145732
  79.9 16.2 %all-to-all-start.4 = ((bf16[4,128,896]{2,1,0:T(8,128)(2,1)}), bf16[4,128,896]{2,1,0:T(8,128)(2,1)S(1)}, u32[]{:S(2)}, u32[]{:S(2)}) async-start(bf16[4,128,896]{2,1,0:T(8,128)(2,1)} %broadcast_in_dim.16), calls=%async_computation.5 | async-start | bytes 1835008 | tf_op jit(solution)/shard_map/all_to_all | solution.py:35
  84.8 106.1 %reduce-scatter.6.cloned.1.call-start = ((), (), s32[]{:S(2)}) async-start(), calls=%async_computation.19 | async-start | bytes 2228224 | tf_op jit(solution)/shard_map/reduce_scatter | solution.py:123
  104.6 1.5 copy-start.11
  109.8 0.7 copy-start.9
  110.5 3.4 copy-start.6
  113.9 1.9 copy-start.12
  113.9 2.1 copy-start.4
  157.0 18.8 %all-to-all-start.3 = ((bf16[8,2,8,4096]{3,2,1,0:T(8,128)(2,1)}), bf16[8,2,8,4096]{3,2,1,0:T(8,128)(2,1)S(1)}, u32[]{:S(2)}, u32[]{:S(2)}) async-start(bf16[8,2,8,4096]{3,2,1,0:T(8,128)(2,1)} %broadcast_in_dim.15), calls=%async_computation.3 | async-start | bytes 2097152 | tf_op jit(solution)/shard_map/all_to_all | solution.py:35
  192.5 11.8 %all-to-all-start.6 = ((bf16[8,128,64]{1,2,0:T(8,128)(2,1)}), bf16[8,128,64]{1,2,0:T(8,128)(2,1)S(1)}, u32[]{:S(2)}, u32[]{:S(2)}) async-start(bf16[8,128,64]{1,2,0:T(8,128)(2,1)} %copy_bitcast_fusion.2), calls=%async_computation.8 | async-start | bytes 262144 | tf_op jit(solution)/shard_map/all_to_all | solution.py:129
  199.1 150.9 %all-gather.2.cloned.1.call-start = ((), (), s32[]{:S(2)}) async-start(), calls=%async_computation.21 | async-start | bytes 2359296 | tf_op jit(solution)/shard_map/all_gather | solution.py:91
  209.0 145.6 %reduce-scatter.8.cloned.1.call-start = ((), (), s32[]{:S(2)}) async-start(), calls=%async_computation.20 | async-start | bytes 8257536 | tf_op jit(solution)/shard_map/reduce_scatter | solution.py:176
  245.4 14.6 %copy-start.5 = (bf16[448,4096]{1,0:T(8,128)(2,1)S(1)}, bf16[448,4096]{1,0:T(8,128)(2,1)}, u32[]{:S(2)}) copy-start(bf16[448,4096]{1,0:T(8,128)(2,1)} %param.14) | copy-start | bytes 11010052
  245.4 14.6 %copy-start.13 = (f32[128,448]{0,1:T(8,128)S(1)}, f32[128,448]{0,1:T(8,128)}, u32[]{:S(2)}) copy-start(f32[128,448]{0,1:T(8,128)} %copy-done.12) | copy-start | bytes 688132
  245.4 14.6 %copy-start.14 = (f32[128,448]{0,1:T(8,128)S(1)}, f32[128,448]{0,1:T(8,128)}, u32[]{:S(2)}) copy-start(f32[128,448]{0,1:T(8,128)} %get-tuple-element.42) | copy-start | bytes 688132
  266.3 3.1 copy-start.7
  271.3 17.7 %all-to-all-start.13 = ((bf16[16,128,256]{2,1,0:T(8,128)(2,1)}), bf16[16,128,256]{2,1,0:T(8,128)(2,1)}, u32[]{:S(2)}, u32[]{:S(2)}) async-start(bf16[16,128,256]{2,1,0:T(8,128)(2,1)} %bitcast.77), calls=%async_computation.16 | async-start | bytes 2097152 | tf_op jit(solution)/shard_map/all_to_all | solution.py:54
  289.0 30.0 %all-to-all-start.12 = ((bf16[128,8,512]{0,2,1:T(8,128)(2,1)}), bf16[128,8,512]{0,2,1:T(8,128)(2,1)S(1)}, u32[]{:S(2)}, u32[]{:S(2)}) async-start(bf16[128,8,512]{0,2,1:T(8,128)(2,1)} %bitcast.76), calls=%async_computation.15 | async-start | bytes 2097152 | tf_op jit(solution)/shard_map/all_to_all | solution.py:172
  319.6 9.8 %all-to-all-start.14 = ((f32[16,128,1]{1,2,0:T(1,128)}), f32[16,128,1]{1,2,0:T(1,128)S(1)}, u32[]{:S(2)}, u32[]{:S(2)}) async-start(f32[16,128,1]{1,2,0:T(1,128)} %broadcast_in_dim.20), calls=%async_computation.17 | async-start | bytes 16384 | tf_op jit(solution)/shard_map/all_to_all | solution.py:35
  329.4 20.5 %all-to-all-start.11 = ((bf16[128,8,512]{2,0,1:T(8,128)(2,1)}), bf16[128,8,512]{2,0,1:T(8,128)(2,1)S(1)}, u32[]{:S(2)}, u32[]{:S(2)}) async-start(bf16[128,8,512]{2,0,1:T(8,128)(2,1)} %copy.64), calls=%async_computation.14 | async-start | bytes 2097152 | tf_op jit(solution)/shard_map/all_to_all | solution.py:173
  338.0 14.8 %copy-start.8 = (bf16[8,128,512]{2,1,0:T(8,128)(2,1)S(1)}, bf16[8,128,512]{2,1,0:T(8,128)(2,1)}, u32[]{:S(2)}) copy-start(bf16[8,128,512]{2,1,0:T(8,128)(2,1)} %copy.66) | copy-start | bytes 3145732
  349.9 2.8 copy-start.10
  352.8 5.3 %copy-start.1 = (bf16[1024,1024]{1,0:T(8,128)(2,1)S(1)}, bf16[1024,1024]{1,0:T(8,128)(2,1)}, u32[]{:S(2)}) copy-start(bf16[1024,1024]{1,0:T(8,128)(2,1)} %param.16) | copy-start | bytes 6291460
Sparse Core Ops, SparseCore 0:
  40.2 37.1 reduce-scatter.3
  110.0 80.8 reduce-scatter.5
  209.2 23.2 all-gather.1
  266.4 57.8 reduce-scatter.7
where the time goes:
time: 366 us; the launch traced here: 365 us
  waiting for transfers between devices  126 us (34%)
  blocking collectives  94.6 us (26%)
  matrix products  41.1 us (11%)
  starting transfers between devices  37.5 us (10%)
  local copies, waits for them, and re-layouts  31.3 us (9%)
  other arithmetic  20 us (5%)
  between operations  14.1 us (4%)
    all_to_all x2, blocking collectives, sent_and_summed(): lax.all_to_all(blocks, axis, split_axis=0, concat_axis=0, tiled=True)  41.2 us
    reduce_scatter x1, waiting for transfers between devices, one_scatter(): lax.psum_scatter(lines, axis, tiled=True).reshape(-1)  37.3 us
    all_to_all x4, blocking collectives, from_everyone(): lax.all_to_all(jnp.broadcast_to(array[None], (peers, *array.shape)), axis...  37.2 us
    all_to_all x3, waiting for transfers between devices, from_everyone(): lax.all_to_all(jnp.broadcast_to(array[None], (peers, *array.shape)), axis...  30.7 us
    all_to_all x1, waiting for transfers between devices, shards(): lax.all_to_all(summed, WID, split_axis=1, concat_axis=0, tiled=True)  17 us
    all_to_all x2, blocking collectives, summed_rows(): lax.all_to_all(nearer.astype(jnp.bfloat16), far, split_axis=0, concat_axi...  16.1 us
    reduce_scatter x1, waiting for transfers between devices, shards(): lax.psum_scatter(feature_part.astype(jnp.bfloat16), GRP_HID, scatter_dime...  13.6 us
    all_to_all x1, waiting for transfers between devices, sent_and_summed(): lax.all_to_all(blocks, axis, split_axis=0, concat_axis=0, tiled=True)  12 us
  transfers between devices with their start and end apart: 11, of which 9 were waited for; matrix products, arithmetic and copies ran while one was open for 11% of the time, Pallas kernels for 0%

commit v1 on v0

v1 whole, which is shorter than its diff:
```python
import jax
import jax.numpy as jnp
from jax import lax
from jax.experimental import pallas as pl
from jax.experimental.pallas import tpu as pltpu
from jax.sharding import Mesh
from jax.sharding import PartitionSpec as P

MESH = pl.DeviceIdType.MESH
F32 = jnp.float32
BF16 = jnp.bfloat16
WID = ("y", "c")
GH = ("zh", "zl", "x")
SEMS = 320

NN = (((1,), (0,)), ((), ()))
NT = (((1,), (1,)), ((), ()))
TN = (((0,), (0,)), ((), ()))


def mm(a, b, dims):
    return lax.dot_general(a, b, dims, preferred_element_type=F32)


def up(v):
    return v.astype(F32)


def mod4(v):
    return lax.rem(v, 4)


class Net:
    def __init__(self, send, recv):
        zh, y, c, zl, x = [lax.axis_index(a) for a in ("zh", "y", "c", "zl", "x")]
        self.z, self.x, self.y, self.c = zh * 2 + zl, x, y, c
        self.send, self.recv, self.copies = send, recv, []

    def at(self, z=None, x=None, y=None, c=None):
        z = self.z if z is None else z
        return {
            "zh": lax.div(z, 2),
            "zl": lax.rem(z, 2),
            "x": self.x if x is None else x,
            "y": self.y if y is None else y,
            "c": self.c if c is None else c,
        }

    def along(self, axis, offset):
        return self.at(**{axis: mod4(getattr(self, axis) + offset)})

    def put(self, src, dst, peer):
        i = len(self.copies)
        copy = pltpu.make_async_remote_copy(
            src_ref=src,
            dst_ref=dst,
            send_sem=self.send.at[i],
            recv_sem=self.recv.at[i],
            device_id=peer,
            device_id_type=MESH,
        )
        copy.start()
        self.copies.append(copy)
        return copy


class RingSum:
    def __init__(self, net, axis, src, buf):
        self.net, self.axis, self.src, self.buf = net, axis, src, buf
        me = getattr(net, axis)
        self.me, self.r, self.o, self.l = me, mod4(me + 1), mod4(me + 2), mod4(me + 3)
        self.right, self.left = net.along(axis, 1), net.along(axis, 3)

    def far(self):
        self.m1 = self.net.put(self.src(self.o, 0), self.buf.at[0], self.right)
        self.n1 = self.net.put(self.src(self.o, 1), self.buf.at[1], self.left)

    def near_r(self):
        self.m2 = self.net.put(self.src(self.r, 1), self.buf.at[2], self.right)

    def near_l(self):
        self.n2 = self.net.put(self.src(self.l, 0), self.buf.at[3], self.left)

    def start(self):
        self.far()
        self.near_r()
        self.near_l()

    def relay(self):
        buf = self.buf
        self.m1.wait_recv()
        buf[0] = (up(buf[0]) + up(self.src(self.r, 0)[...])).astype(BF16)
        self.m3 = self.net.put(buf.at[0], buf.at[4], self.right)
        self.n1.wait_recv()
        buf[1] = (up(buf[1]) + up(self.src(self.l, 1)[...])).astype(BF16)
        self.n3 = self.net.put(buf.at[1], buf.at[5], self.left)

    def finish(self):
        buf = self.buf
        self.n2.wait_recv()
        self.m3.wait_recv()
        first = up(self.src(self.me, 0)[...]) + up(buf[3]) + up(buf[4])
        self.m2.wait_recv()
        self.n3.wait_recv()
        second = up(self.src(self.me, 1)[...]) + up(buf[2]) + up(buf[5])
        return first, second


class PlaneSum:
    def __init__(self, net, j, data, q, buf1, mid, buf2):
        self.net, self.mid = net, mid
        if j == 0:
            src, axes = (lambda d, h: data.at[:, d, q[h]]), ("x", "z")
        else:
            src, axes = (lambda d, h: data.at[d, :, q[h]]), ("z", "x")
        self.one = RingSum(net, axes[0], src, buf1)
        self.two = RingSum(net, axes[1], lambda d, h: mid.at[h, d], buf2)

    def start(self):
        self.one.start()

    def relay1(self):
        self.one.relay()

    def turn(self):
        first, second = self.one.finish()
        self.mid[0] = first.astype(BF16)
        self.mid[1] = second.astype(BF16)
        self.two.start()

    def relay2(self):
        self.two.relay()

    def finish(self):
        return self.two.finish()


class RingAll:
    def __init__(self, net, axis, whole, part):
        self.net, self.whole, self.part = net, whole, part
        me = getattr(net, axis)
        self.me, self.r, self.l = me, mod4(me + 1), mod4(me + 3)
        self.right, self.left = net.along(axis, 1), net.along(axis, 3)

    def start(self):
        own = self.whole(self.me)
        self.m1 = self.net.put(own, own, self.right)
        self.n1 = self.net.put(own, own, self.left)

    def relay(self):
        self.m1.wait_recv()
        piece = self.part(self.l, 0)
        self.m2 = self.net.put(piece, piece, self.right)
        self.n1.wait_recv()
        piece = self.part(self.r, 1)
        self.n2 = self.net.put(piece, piece, self.left)

    def finish(self):
        self.m2.wait_recv()
        self.n2.wait_recv()


class PlaneAll:
    def __init__(self, net, data):
        z, x = net.z, net.x
        self.a1 = RingAll(
            net, "z", lambda d: data.at[d, x, pl.ds(0, 2)], lambda d, h: data.at[d, x, h]
        )
        self.b1 = RingAll(
            net, "x", lambda d: data.at[z, d, pl.ds(2, 2)], lambda d, h: data.at[z, d, 2 + h]
        )
        self.a2 = RingAll(
            net, "x", lambda d: data.at[:, d, pl.ds(0, 2)], lambda d, h: data.at[:, d, h]
        )
        self.b2 = RingAll(
            net, "z", lambda d: data.at[d, :, pl.ds(2, 2)], lambda d, h: data.at[d, :, 2 + h]
        )

    def start(self):
        self.a1.start()
        self.b1.start()

    def relay1(self):
        self.a1.relay()
        self.b1.relay()

    def turn(self):
        self.a1.finish()
        self.a2.start()
        self.b1.finish()
        self.b2.start()

    def relay2(self):
        self.a2.relay()
        self.b2.relay()

    def finish(self):
        self.a2.finish()
        self.b2.finish()


class TokenAll:
    def __init__(self, net, data):
        rows = data.shape[0]
        self.net, self.data = net, data

        def slot(d, c, h=None):
            at = pl.multiple_of((d * 2 + c) * 128, 128)
            if h is None:
                return data.at[:, pl.ds(at, 128)]
            return data.at[pl.ds(h * (rows // 2), rows // 2), pl.ds(at, 128)]

        self.slot = slot
        self.ring = RingAll(
            net, "y", lambda d: slot(d, net.c), lambda d, h: slot(d, net.c, h)
        )
        self.own = slot(net.y, net.c)
        self.mate = net.at(c=1 - net.c)
        self.mates = {}

    def share(self, offset):
        piece = self.slot(mod4(self.net.y + offset), self.net.c)
        self.mates[offset] = self.net.put(piece, piece, self.mate)

    def start(self):
        self.ring.start()
        self.share(0)

    def relay(self):
        self.ring.relay()
        self.share(1)
        self.share(3)

    def finish(self):
        self.ring.finish()
        self.share(2)

    def wait(self, offset):
        self.mates[offset].wait_recv()


class Columns:
    def __init__(self, net, source, data):
        self.net, self.source, self.data = net, source, data
        self.plane = PlaneAll(net, data)

    def spread(self):
        net = self.net
        rows = pl.ds(pl.multiple_of(lax.div(net.x, 2) * 16, 16), 16)
        half = lax.rem(net.x, 2)
        to = self.data.at[net.z, net.x, net.y, pl.ds(pl.multiple_of(net.c * 16, 16), 16)]

        def piece(y, c):
            return self.source.at[y, 2 * c + half, net.z, rows]

        to[...] = piece(net.y, net.c)[...]
        self.copies = []
        for offset in (2, 1, 3, 0):
            for flip in (0, 1):
                if offset or flip:
                    y, c = mod4(net.y + offset), lax.rem(net.c + flip, 2)
                    self.copies.append(net.put(piece(y, c), to, net.at(y=y, c=c)))

    def start(self):
        for copy in self.copies:
            copy.wait_recv()
        self.plane.start()

    def unpack(self, out):
        data = self.data

        def body(y, _):
            for c in (0, 1):
                for half in (0, 1):
                    parts = [
                        data[z, 2 * i + half, y, 16 * c : 16 * c + 16]
                        for z in range(4)
                        for i in (0, 1)
                    ]
                    at = pl.multiple_of(y * 256 + c * 128, 128)
                    out[pl.ds(at, 128), 256 * half : 256 * half + 256] = jnp.concatenate(
                        parts, axis=0
                    )
            return 0

        lax.fori_loop(0, 4, body, 0)


def share_of(ref, z, x):
    return ref[z, x].reshape(128, 256)


def wide_of(ref, z):
    return jnp.concatenate([share_of(ref, z, x) for x in range(4)], axis=1)


def kernel(
    student_in,
    norm_gain,
    gate_weight,
    up_weight,
    down_weight,
    projection,
    teacher_in,
    teacher_gate,
    teacher_up,
    teacher_down,
    grad_gate,
    grad_up,
    grad_down,
    grad_proj,
    input_grad,
    xin,
    gain,
    wg,
    wu,
    wd,
    pj,
    tin,
    tg,
    tu,
    td,
    tdt,
    parts,
    mate,
    ring,
    thid,
    feat,
    feat1,
    featm,
    feat2,
    sums,
    sums1,
    summ,
    sums2,
    normed,
    summed,
    bgrad,
    ncols,
    scols,
    bcols,
    flat,
    hids,
    errs,
    ggs,
    gate,
    upsum,
    sigma,
    acc,
    acc2,
    tshare,
    target,
    fgrad,
    stat,
    statx,
    statz,
    invs,
    load,
    send,
    recv,
):
    net = Net(send, recv)
    z, x, y, c = net.z, net.x, net.y, net.c
    ys = [mod4(y + o) for o in range(4)]

    loads = {}
    for i, (name, src, dst) in enumerate(
        (
            ("xin", student_in, xin),
            ("gain", norm_gain, gain),
            ("tin", teacher_in, tin),
            ("tg", teacher_gate, tg),
            ("tu", teacher_up, tu),
            ("wg", gate_weight, wg),
            ("wu", up_weight, wu),
            ("wd", down_weight, wd),
            ("td", teacher_down, td),
            ("pj", projection, pj),
        )
    ):
        loads[name] = pltpu.make_async_copy(src, dst, load.at[i])
        loads[name].start()

    barrier = pltpu.get_barrier_semaphore()
    peers = [net.at(y=mod4(y + o), c=lax.rem(c + f, 2)) for o in range(4) for f in (0, 1) if o or f]
    peers += [net.along("x", o) for o in (1, 2, 3)] + [net.along("z", o) for o in (1, 2, 3)]
    for peer in peers:
        pl.semaphore_signal(barrier, inc=1, device_id=peer, device_id_type=MESH)

    loads["xin"].wait()
    loads["gain"].wait()

    def squares(b, total):
        v = up(xin[:, pl.ds(pl.multiple_of(b * 256, 256), 256)])
        return total + v * v

    total = lax.fori_loop(0, 16, squares, jnp.zeros((128, 256), F32))
    inv = lax.rsqrt(jnp.sum(total, axis=1, keepdims=True) / 4096.0 + 1e-05)
    invs[...] = jnp.broadcast_to(inv, (128, 128))

    def norm(b, _):
        at = pl.ds(pl.multiple_of(b * 256, 256), 256)
        scale = jnp.concatenate([invs[...], invs[...]], axis=1)
        v = up(xin[:, at]) * scale * gain[:, at]
        normed[lax.div(b, 4), lax.rem(b, 4)] = v.astype(BF16).reshape(4, 32, 256)
        return 0

    lax.fori_loop(0, 16, norm, 0)
    pl.semaphore_wait(barrier, len(peers))
    ncol = Columns(net, normed, ncols)
    ncol.spread()

    tsum = RingSum(
        net, "y", lambda d, h: parts.at[d, c, pl.ds(64 * h, 64)], ring
    )
    for name in ("tin", "tg", "tu"):
        loads[name].wait()
    pair = {}

    def project(o):
        d = ys[o]
        rows = tin[pl.ds(pl.multiple_of(d * 256, 256), 256), :]
        parts[d, :, :, 0:896] = mm(rows, tg[...], NN).astype(BF16).reshape(2, 128, 896)
        parts[d, :, :, 896:1792] = mm(rows, tu[...], NN).astype(BF16).reshape(2, 128, 896)

    def swap(o):
        d = ys[o]
        pair[o] = net.put(parts.at[d, 1 - c], mate.at[d], net.at(c=1 - c))

    def join(o):
        d = ys[o]
        pair[o].wait_recv()
        parts[d, c] = (up(parts[d, c]) + up(mate[d])).astype(BF16)

    project(2)
    swap(2)
    ncol.start()
    project(1)
    swap(1)
    join(2)
    tsum.far()
    ncol.plane.relay1()
    project(3)
    swap(3)
    join(1)
    tsum.near_r()
    ncol.plane.turn()
    project(0)
    swap(0)
    join(3)
    tsum.near_l()
    ncol.plane.relay2()

    for name in ("wg", "wu", "wd"):
        loads[name].wait()

    def students(first, second, source, out_first, out_second):
        def body(b, _):
            at = pl.ds(pl.multiple_of(b * 1024, 1024), 1024)
            wide = wide_of(source, b)
            out_first[...] += mm(first[:, at], wide, NT)
            if second is not None:
                out_second[...] += mm(second[:, at], wide, NT)
            return 0

        out_first[...] = jnp.zeros(out_first.shape, F32)
        if second is not None:
            out_second[...] = jnp.zeros(out_second.shape, F32)
        lax.fori_loop(0, 4, body, 0)

    def back(out, pairs):
        def body(b, _):
            at = pl.ds(pl.multiple_of(b * 1024, 1024), 1024)
            v = sum(mm(small, w[:, at], TN) for small, w in pairs).astype(BF16)
            for i in range(4):
                out[b, i] = v[:, 256 * i : 256 * i + 256].reshape(4, 32, 256)
            return 0

        lax.fori_loop(0, 4, body, 0)

    students(wg, wu, normed, gate, upsum)
    tsum.relay()
    sig = jax.nn.sigmoid(gate[...])
    sigma[...] = sig
    hid = (gate[...] * sig * upsum[...]).astype(BF16)
    hiddens = TokenAll(net, hids)
    hiddens.own[...] = hid

    def plane_sums(n):
        return [
            PlaneSum(
                net, j, sums.at[n], (2 * j, 2 * j + 1), sums1.at[n, j], summ.at[n, j], sums2.at[n, j]
            )
            for j in (0, 1)
        ]

    back(sums.at[0], ((hid, wd),))
    branch = plane_sums(0)
    for s in branch:
        s.start()

    loads["td"].wait()
    tdt[...] = td[...].T
    join(0)
    ncol.plane.finish()
    for s in branch:
        s.relay1()

    first, second = tsum.finish()
    sums_all = jnp.concatenate([first, second], axis=0)
    g = sums_all[:, :896]
    teach = g * jax.nn.sigmoid(g) * sums_all[:, 896:]
    teachers = TokenAll(net, thid)
    teachers.own[...] = teach.T.astype(BF16)
    teachers.start()
    for s in branch:
        s.turn()

    order = [ys[0], ys[1], ys[3], ys[2]]

    def feature(o):
        d = ys[o]
        teachers.wait(o)
        v = mm(tdt[...], thid[:, pl.ds(pl.multiple_of(d * 256, 256), 256)], NN).astype(BF16)
        for f in (0, 1):
            feat[:, :, d, 64 * f : 64 * f + 64] = v[:, 128 * f : 128 * f + 128].reshape(
                4, 4, 64, 128
            )

    teaching = [
        PlaneSum(net, j, feat, (order[2 * j], order[2 * j + 1]), feat1.at[j], featm.at[j], feat2.at[j])
        for j in (0, 1)
    ]
    feature(0)
    for s in branch:
        s.relay2()
    teachers.relay()
    feature(1)
    teaching[0].start()

    rows_of = lambda q: pl.ds(32 * q, 32)
    share_at = pl.ds(pl.multiple_of((z * 4 + x) * 256, 256), 256)
    for j in (0, 1):
        for h, v in enumerate(branch[j].finish()):
            q = 2 * j + h
            summed[z, x, q] = (up(xin[rows_of(q), share_at]) + v).astype(BF16)
    sum_all = PlaneAll(net, summed)
    sum_all.start()
    feature(3)
    teachers.finish()
    sum_all.relay1()
    teaching[0].relay1()
    feature(2)
    teaching[1].start()
    hiddens.start()
    sum_all.turn()
    teaching[0].turn()
    teaching[1].relay1()
    sum_all.relay2()
    teaching[0].relay2()
    teaching[1].turn()
    hiddens.relay()
    sum_all.finish()
    scol = Columns(net, summed, scols)
    scol.spread()
    loads["pj"].wait()
    students(pj, None, summed, acc, None)

    sent = []

    def hand(k, v):
        d = order[k]
        tshare[d] = v.astype(BF16)
        to = target.at[pl.ds(pl.multiple_of((y * 2 + c) * 64, 64), 64)]
        for f in (0, 1):
            cc = lax.rem(c + f, 2)
            piece = tshare.at[d, pl.ds(pl.multiple_of(cc * 64, 64), 64)]
            if k == 0 and f == 0:
                to[...] = piece[...]
            else:
                sent.append(net.put(piece, to, net.at(y=d, c=cc)))

    for k, v in enumerate(teaching[0].finish()):
        hand(k, v)
    teaching[1].relay2()
    for k, v in enumerate(teaching[1].finish()):
        hand(2 + k, v)
    scol.start()
    hiddens.finish()
    scol.plane.relay1()
    for copy in sent:
        copy.wait_recv()

    err = ((acc[...] - up(target[...])) * (1.0 / 32.0)).astype(BF16)
    errors = TokenAll(net, errs)
    errors.own[...] = err
    errors.start()
    back(sums.at[1], ((err, pj),))
    grads = plane_sums(1)
    for s in grads:
        s.start()
    scol.plane.turn()
    for s in grads:
        s.relay1()
    errors.relay()
    scol.plane.relay2()
    for s in grads:
        s.turn()
    errors.finish()
    for o in (1, 3, 2):
        hiddens.wait(o)
    hiddens.wait(0)
    for s in grads:
        s.relay2()
    for j in (0, 1):
        for h, v in enumerate(grads[j].finish()):
            q = 2 * j + h
            fgrad[rows_of(q), :] = v
            bgrad[z, x, q] = v.astype(BF16)
    grad_all = PlaneAll(net, bgrad)
    grad_all.start()
    scol.plane.finish()
    scol.unpack(flat)
    grad_all.relay1()
    for o in range(4):
        errors.wait(o)
    grad_proj[0:256] = mm(errs[0:256], flat[...], NN).astype(BF16)
    grad_all.turn()
    grad_proj[256:512] = mm(errs[256:512], flat[...], NN).astype(BF16)
    ncol.unpack(flat)
    grad_all.relay2()
    grad_all.finish()
    bcol = Columns(net, bgrad, bcols)
    bcol.spread()

    students(wd, None, bgrad, acc2, None)
    hg = acc2[...]
    g, s = gate[...], sigma[...]
    gg = (hg * upsum[...] * s * (1.0 + g * (1.0 - s))).astype(BF16)
    ug = (hg * g * s).astype(BF16)
    moment = jnp.sum(up(gg) * g + up(ug) * upsum[...], axis=0, keepdims=True)
    gates = TokenAll(net, ggs)
    ggs[0:448, pl.ds(pl.multiple_of((y * 2 + c) * 128, 128), 128)] = gg
    ggs[448:896, pl.ds(pl.multiple_of((y * 2 + c) * 128, 128), 128)] = ug
    gates.start()
    statx[x] = jnp.broadcast_to(moment, (8, 128))
    stats = [net.put(statx.at[x], statx.at[x], net.along("x", o)) for o in (1, 2, 3)]
    back(sums.at[2], ((gg, wg), (ug, wu)))
    inner = plane_sums(2)
    for s in inner:
        s.start()
    for copy in stats:
        copy.wait_recv()
    statz[z] = statx[0] + statx[1] + statx[2] + statx[3]
    stats = [net.put(statz.at[z], statz.at[z], net.along("z", o)) for o in (1, 2, 3)]
    bcol.start()
    for s in inner:
        s.relay1()
    bcol.plane.relay1()
    for s in inner:
        s.turn()
    gates.relay()
    bcol.plane.turn()
    for copy in stats:
        copy.wait_recv()
    whole = (statz[0] + statz[1] + statz[2] + statz[3]) / 4096.0
    stat[...] = jnp.broadcast_to(whole[0:1], (128, 128)).T
    for s in inner:
        s.relay2()
    gates.finish()
    bcol.plane.relay2()
    for j in (0, 1):
        for h, v in enumerate(inner[j].finish()):
            r = rows_of(2 * j + h)
            scale = jnp.concatenate([invs[r, :], invs[r, :]], axis=1)
            mean = jnp.concatenate([stat[r, :], stat[r, :]], axis=1)
            scaled = v * gain[:, share_at]
            input_grad[r, :] = fgrad[r, :] + scale * (
                scaled - up(xin[r, share_at]) * scale * mean
            )
    for o in range(4):
        gates.wait(o)
    grad_gate[...] = mm(ggs[0:448], flat[...], NN).astype(BF16)
    grad_up[...] = mm(ggs[448:896], flat[...], NN).astype(BF16)
    bcol.plane.finish()
    bcol.unpack(flat)
    grad_down[...] = mm(hids[...], flat[...], NN).astype(BF16)
    for copy in net.copies:
        copy.wait_send()


def shards(
    student_in,
    norm_gain,
    gate_weight,
    up_weight,
    down_weight,
    projection,
    teacher_in,
    teacher_gate,
    teacher_up,
    teacher_down,
):
    vmem = pltpu.VMEM
    anyspec = pl.BlockSpec(memory_space=pl.ANY)
    out = pl.BlockSpec(memory_space=pltpu.VMEM)
    gg, gu, gd, gp, ig = pl.pallas_call(
        kernel,
        out_shape=(
            jax.ShapeDtypeStruct((448, 512), BF16),
            jax.ShapeDtypeStruct((448, 512), BF16),
            jax.ShapeDtypeStruct((448, 512), BF16),
            jax.ShapeDtypeStruct((512, 512), BF16),
            jax.ShapeDtypeStruct((128, 256), F32),
        ),
        in_specs=[anyspec] * 10,
        out_specs=(out,) * 5,
        scratch_shapes=[
            vmem((128, 4096), BF16),
            vmem((1, 4096), F32),
            vmem((448, 4096), BF16),
            vmem((448, 4096), BF16),
            vmem((448, 4096), BF16),
            vmem((512, 4096), BF16),
            vmem((1024, 1024), BF16),
            vmem((1024, 896), BF16),
            vmem((1024, 896), BF16),
            vmem((896, 1024), BF16),
            vmem((1024, 896), BF16),
            vmem((4, 2, 128, 1792), BF16),
            vmem((4, 128, 1792), BF16),
            vmem((6, 64, 1792), BF16),
            vmem((896, 1024), BF16),
            vmem((4, 4, 4, 128, 128), BF16),
            vmem((2, 6, 4, 128, 128), BF16),
            vmem((2, 2, 4, 128, 128), BF16),
            vmem((2, 6, 128, 128), BF16),
            vmem((3, 4, 4, 4, 32, 256), BF16),
            vmem((3, 2, 6, 4, 32, 256), BF16),
            vmem((3, 2, 2, 4, 32, 256), BF16),
            vmem((3, 2, 6, 32, 256), BF16),
            vmem((4, 4, 4, 32, 256), BF16),
            vmem((4, 4, 4, 32, 256), BF16),
            vmem((4, 4, 4, 32, 256), BF16),
            vmem((4, 4, 4, 32, 256), BF16),
            vmem((4, 4, 4, 32, 256), BF16),
            vmem((4, 4, 4, 32, 256), BF16),
            vmem((1024, 512), BF16),
            vmem((448, 1024), BF16),
            vmem((512, 1024), BF16),
            vmem((896, 1024), BF16),
            vmem((448, 128), F32),
            vmem((448, 128), F32),
            vmem((448, 128), F32),
            vmem((512, 128), F32),
            vmem((448, 128), F32),
            vmem((4, 128, 128), BF16),
            vmem((512, 128), BF16),
            vmem((128, 256), F32),
            vmem((128, 128), F32),
            vmem((4, 8, 128), F32),
            vmem((4, 8, 128), F32),
            vmem((128, 128), F32),
            pltpu.SemaphoreType.DMA((10,)),
            pltpu.SemaphoreType.DMA((SEMS,)),
            pltpu.SemaphoreType.DMA((SEMS,)),
        ],
        compiler_params=pltpu.CompilerParams(
            collective_id=0, has_side_effects=True, vmem_limit_bytes=67043328
        ),
    )(
        student_in,
        norm_gain.reshape(1, -1),
        gate_weight.T,
        up_weight.T,
        down_weight,
        projection.transpose(1, 2, 0).reshape(512, -1),
        teacher_in,
        teacher_gate,
        teacher_up,
        teacher_down,
    )
    return gg.T, gu.T, gd, gp.reshape(8, 64, 512).transpose(2, 0, 1), ig


def solution(mesh):
    split = Mesh(mesh.devices.reshape(2, 4, 2, 2, 4), ("zh", "y", "c", "zl", "x"))
    in_specs = (
        P(WID, None),
        P(),
        P(None, GH),
        P(None, GH),
        P(GH, None),
        P(None, None, GH),
        P(None, WID),
        P(WID, GH),
        P(WID, GH),
        P(GH, WID),
    )
    out_specs = (
        P(WID, GH),
        P(WID, GH),
        P(GH, WID),
        P(WID, None, GH),
        P(WID, GH),
    )
    return jax.shard_map(
        shards, mesh=split, in_specs=in_specs, out_specs=out_specs, check_vma=False
    )
```

time: 366 us -> 148 us (0.40)
  Pallas kernels: 0 us -> 138 us
  waiting for transfers between devices: 126 us -> 0 us
  blocking collectives: 94.6 us -> 0 us
  matrix products: 41.1 us -> 0 us
  starting transfers between devices: 37.5 us -> 0 us
  local copies, waits for them, and re-layouts: 31.3 us -> 8.01 us
  other arithmetic: 20 us -> 0 us
  between operations: 14.1 us -> 0.65 us
    pallas_call x0 -> x1, Pallas kernels: none -> 138 us  [shards(): pl.pallas_call(kernel, out_shape=(jax.ShapeDtypeStruct((448, 512), BF16),...]
    all_to_all x8 -> x0, blocking collectives: 94.6 us -> none  [the longest x2 41.2 us: sent_and_summed(): lax.all_to_all(blocks, axis, split_axis=0, concat_axis=0, tiled=True)]
    all_to_all x7 -> x0, waiting for transfers between devices: 75 us -> none  [the longest x3 30.7 us: from_everyone(): lax.all_to_all(jnp.broadcast_to(array[None], (peers, *array.shape)), axis...]
    reduce_scatter x3 -> x0, waiting for transfers between devices: 50.9 us -> none  [the longest x1 37.3 us: one_scatter(): lax.psum_scatter(lines, axis, tiled=True).reshape(-1)]
    dot_general x14 -> x0, matrix products: 41.1 us -> none  [the longest x1 5.13 us: shards(): jnp.dot(normed.T, paired_grad, preferred_element_type=f32)]
    all_to_all x7 -> x0, starting transfers between devices: 37.4 us -> none  [the longest x3 12 us: from_everyone(): lax.all_to_all(jnp.broadcast_to(array[None], (peers, *array.shape)), axis...]
    concatenate x2 -> x0, other arithmetic: 9.17 us -> none  [the longest x1 8.34 us: one_scatter(): lines = jnp.concatenate([b.reshape(peers, -1) for b in blocks], axis=1)]
    another operation x4 -> x0, local copies, waits for them, and re-layouts: 7.47 us -> none  [the longest x2 7.31 us: one_scatter(): lines = jnp.concatenate([b.reshape(peers, -1) for b in blocks], axis=1)]
  transfers between devices with their start and end apart: 11 -> 0, of which waited for: 9 -> 0; matrix products, arithmetic and copies ran while one was open for 11% -> 0% of each run, Pallas kernels for 0% -> 0%
where the time goes in v1:
time: 148 us; the launch traced here: 146 us
  Pallas kernels  138 us (93%)
  local copies, waits for them, and re-layouts  8.01 us (5%)
    pallas_call x1, Pallas kernels, shards(): pl.pallas_call(kernel, out_shape=(jax.ShapeDtypeStruct((448, 512), BF16),...  138 us
    unnamed x7, local copies, waits for them, and re-layouts  8.01 us

profile of v1, /device:TPU:1, one launch (start us, length us, event | category | flops | bytes accessed | tf_op | source)
XLA Modules:
  0.0 146.2 jit_solution(12075227455332991038)
XLA Ops:
  0.6 137.6 %shard_map.137 = (bf16[448,512]{1,0:T(8,128)(2,1)}, bf16[448,512]{1,0:T(8,128)(2,1)}, bf16[448,512]{1,0:T(8,128)(2,1)}, bf16[512,512]{1,0:T(8,128)(2,1)}, f32[128,256]{1,0:T(8,128)}) custom-call(bf16[128,4096]{1,0:T(8,128)(2,1)} %student_in.1, f32[1,4096]{1,0:T(1,128)} %bitcast.17, bf16[448,4096]{1,0:T(8,128)(2,1)} %bitcast.12, bf16[448,4096]{1,0:T(8,128)(2,1)} %bitcast.13, ...), custom_call_target="tpu_custom_call" | custom-call | tf_op jit(solution)/shard_map/pallas_call | solution.py:707
  138.2 0.0 copy-start
  138.2 1.9 %copy.20 = bf16[512,448]{0,1:T(8,128)(2,1)} copy(bf16[512,448]{0,1:T(8,128)(2,1)} %bitcast.16) | data formatting | bytes 917504
  140.1 1.8 %copy.21 = bf16[512,448]{0,1:T(8,128)(2,1)} copy(bf16[512,448]{0,1:T(8,128)(2,1)} %bitcast.15) | data formatting | bytes 917504
  141.9 1.8 %copy.22 = bf16[448,512]{1,0:T(8,128)(2,1)} copy(bf16[448,512]{1,0:T(8,128)(2,1)} %get-tuple-element.22) | data formatting | bytes 917504
  143.7 1.9 %copy.23 = bf16[512,8,64]{0,2,1:T(8,128)(2,1)} copy(bf16[512,8,64]{0,2,1:T(8,128)(2,1)} %bitcast.14) | data formatting | bytes 1048576
  145.6 0.0 copy-done
  145.6 0.7 copy.24
Async XLA Ops:
  138.2 7.4 %copy-start = (f32[128,256]{1,0:T(8,128)S(1)}, f32[128,256]{1,0:T(8,128)}, u32[]{:S(2)}) copy-start(f32[128,256]{1,0:T(8,128)} %get-tuple-element.24) | copy-start | bytes 393220

commit v2 on v1

v2 whole, which is shorter than its diff:
```python
import jax
import jax.numpy as jnp
from jax import lax
from jax.experimental import pallas as pl
from jax.experimental.pallas import tpu as pltpu
from jax.sharding import Mesh
from jax.sharding import PartitionSpec as P

MESH = pl.DeviceIdType.MESH
F32 = jnp.float32
BF16 = jnp.bfloat16
WID = ("y", "c")
GH = ("zh", "zl", "x")
SEMS = 86

NN = (((1,), (0,)), ((), ()))
NT = (((1,), (1,)), ((), ()))
TN = (((0,), (0,)), ((), ()))


def mm(a, b, dims):
    return lax.dot_general(a, b, dims, preferred_element_type=F32)


def up(v):
    return v.astype(F32)


def mod4(v):
    return lax.rem(v, 4)


class Net:
    def __init__(self, send, recv):
        zh, y, c, zl, x = [lax.axis_index(a) for a in ("zh", "y", "c", "zl", "x")]
        self.z, self.x, self.y, self.c = zh * 2 + zl, x, y, c
        self.send, self.recv, self.copies, self.count = send, recv, [], 0

    def at(self, z=None, x=None, y=None, c=None):
        z = self.z if z is None else z
        return {
            "zh": lax.div(z, 2),
            "zl": lax.rem(z, 2),
            "x": self.x if x is None else x,
            "y": self.y if y is None else y,
            "c": self.c if c is None else c,
        }

    def along(self, axis, offset):
        return self.at(**{axis: mod4(getattr(self, axis) + offset)})

    def make(self, src, dst, peer, i):
        return pltpu.make_async_remote_copy(
            src_ref=src,
            dst_ref=dst,
            send_sem=self.send.at[i],
            recv_sem=self.recv.at[i],
            device_id=peer,
            device_id_type=MESH,
        )

    def slots(self, n):
        self.count += n
        return self.count - n

    def put(self, src, dst, peer):
        copy = self.make(src, dst, peer, self.slots(1))
        copy.start()
        self.copies.append(copy)
        return copy

    def group(self, size):
        whole = self.make(size, size, self.at(c=1 - self.c), self.slots(1))
        self.copies.append(whole)
        return Group(self, whole, self.count - 1)


class Group:
    def __init__(self, net, whole, i):
        self.net, self.whole, self.i = net, whole, i

    def put(self, src, dst, peer):
        self.net.make(src, dst, peer, self.i).start()

    def wait_recv(self):
        self.whole.wait_recv()


class RingSum:
    def __init__(self, net, axis, src, buf):
        self.net, self.axis, self.src, self.buf = net, axis, src, buf
        me = getattr(net, axis)
        self.me, self.r, self.o, self.l = me, mod4(me + 1), mod4(me + 2), mod4(me + 3)
        self.right, self.left = net.along(axis, 1), net.along(axis, 3)

    def far(self):
        self.m1 = self.net.put(self.src(self.o, 0), self.buf.at[0], self.right)
        self.n1 = self.net.put(self.src(self.o, 1), self.buf.at[1], self.left)

    def near_r(self):
        self.m2 = self.net.put(self.src(self.r, 1), self.buf.at[2], self.right)

    def near_l(self):
        self.n2 = self.net.put(self.src(self.l, 0), self.buf.at[3], self.left)

    def start(self):
        self.far()
        self.near_r()
        self.near_l()

    def relay(self):
        buf = self.buf
        self.m1.wait_recv()
        buf[0] = (up(buf[0]) + up(self.src(self.r, 0)[...])).astype(BF16)
        self.m3 = self.net.put(buf.at[0], buf.at[4], self.right)
        self.n1.wait_recv()
        buf[1] = (up(buf[1]) + up(self.src(self.l, 1)[...])).astype(BF16)
        self.n3 = self.net.put(buf.at[1], buf.at[5], self.left)

    def finish(self):
        buf = self.buf
        self.n2.wait_recv()
        self.m3.wait_recv()
        first = up(self.src(self.me, 0)[...]) + up(buf[3]) + up(buf[4])
        self.m2.wait_recv()
        self.n3.wait_recv()
        second = up(self.src(self.me, 1)[...]) + up(buf[2]) + up(buf[5])
        return first, second


class PlaneSum:
    def __init__(self, net, axes, src, buf1, mid, buf2):
        self.net, self.axes, self.src = net, axes, src
        self.buf1, self.mid, self.buf2 = buf1, mid, buf2

    def deal(self, axis, src, buf):
        me = getattr(self.net, axis)
        group = self.net.group(buf)
        for o in (2, 1, 3):
            group.put(src(mod4(me + o)), buf.at[o - 1], self.net.along(axis, o))
        return group

    def total(self, group, own, buf):
        group.wait_recv()
        return up(own[...]) + up(buf[0]) + up(buf[1]) + up(buf[2])

    def start(self):
        self.one = self.deal(self.axes[0], self.src, self.buf1)

    def turn(self):
        me = getattr(self.net, self.axes[0])
        self.mid[...] = self.total(self.one, self.src(me), self.buf1).astype(BF16)
        self.second()

    def second(self):
        self.two = self.deal(self.axes[1], lambda d: self.mid.at[d], self.buf2)

    def finish(self):
        me = getattr(self.net, self.axes[1])
        return self.total(self.two, self.mid.at[me], self.buf2)


class PlaneAll:
    def __init__(self, net, data, sizes):
        self.net, self.data, self.sizes = net, data, sizes

    def copies(self, piece, axis, size):
        group = self.net.group(size)
        for o in (2, 1, 3):
            group.put(piece, piece, self.net.along(axis, o))
        return group

    def start(self):
        z, x, size = self.net.z, self.net.x, self.sizes[0]
        self.a = self.copies(self.data.at[z, x, pl.ds(0, 2)], "z", size)
        self.b = self.copies(self.data.at[z, x, pl.ds(2, 2)], "x", size)

    def turn(self):
        z, x, size = self.net.z, self.net.x, self.sizes[1]
        self.a.wait_recv()
        self.a = self.copies(self.data.at[:, x, pl.ds(0, 2)], "x", size)
        self.b.wait_recv()
        self.b = self.copies(self.data.at[z, :, pl.ds(2, 2)], "z", size)

    def finish(self):
        self.a.wait_recv()
        self.b.wait_recv()


class TokenDirect:
    def __init__(self, net, data):
        self.net, self.data = net, data
        self.own = self.slot(0)

    def slot(self, o):
        at = pl.multiple_of((mod4(self.net.y + o) * 2 + self.net.c) * 128, 128)
        return self.data.at[:, pl.ds(at, 128)]

    def start(self):
        net, own = self.net, self.own
        self.mate = net.at(c=1 - net.c)
        self.far = [(4 - o, net.put(own, own, net.along("y", o))) for o in (2, 1, 3)]
        self.near = [net.put(own, own, self.mate)]

    def pass_on(self):
        for o, copy in self.far:
            copy.wait_recv()
            piece = self.slot(o)
            self.near.append(self.net.put(piece, piece, self.mate))

    def finish(self):
        for copy in self.near:
            copy.wait_recv()


class TokenAll:
    def __init__(self, net, data):
        self.net, self.data, self.rows = net, data, data.shape[0]
        self.own = self.slot(0)
        self.mate = net.at(c=1 - net.c)
        self.mates = {}

    def slot(self, o, h=None):
        at = pl.multiple_of((mod4(self.net.y + o) * 2 + self.net.c) * 128, 128)
        if h is None:
            return self.data.at[:, pl.ds(at, 128)]
        half = self.rows // 2
        return self.data.at[pl.ds(h * half, half), pl.ds(at, 128)]

    def send(self, o, h, to):
        piece = self.slot(o, h)
        return self.net.put(piece, piece, self.net.along("y", to))

    def share(self, o):
        piece = self.slot(o)
        self.mates[o] = self.net.put(piece, piece, self.mate)

    def start(self):
        self.share(0)
        self.r0, self.l1 = self.send(0, 0, 1), self.send(0, 1, 3)
        self.r1, self.l0 = self.send(0, 1, 1), self.send(0, 0, 3)

    def relay(self):
        self.r0.wait_recv()
        self.rr = self.send(3, 0, 1)
        self.l1.wait_recv()
        self.ll = self.send(1, 1, 3)

    def near(self):
        self.l0.wait_recv()
        self.share(1)
        self.r1.wait_recv()
        self.share(3)

    def finish(self):
        self.rr.wait_recv()
        self.ll.wait_recv()
        self.share(2)

    def wait(self, o):
        self.mates[o].wait_recv()


class Direct:
    def __init__(self, net, source, data):
        self.net, self.source, self.data = net, source, data

        self.group = net.group(data.at[pl.ds(0, 7)])

    def start(self, offsets):
        net = self.net
        to = self.data.at[net.y * 2 + net.c]
        if 0 in offsets:
            to[...] = self.source[net.y, pl.ds(2 * net.c, 2)]
        for o in offsets:
            for flip in (0, 1):
                if o or flip:
                    y, c = mod4(net.y + o), lax.rem(net.c + flip, 2)
                    piece = self.source.at[y, pl.ds(2 * c, 2)]
                    self.group.put(piece, to, net.at(y=y, c=c))

    def unpack(self, out):
        self.group.wait_recv()

        def body(w, _):
            rows = pl.ds(pl.multiple_of(w * 128, 128), 128)
            for half in (0, 1):
                out[rows, 256 * half : 256 * half + 256] = self.data[w, half].reshape(128, 256)
            return 0

        lax.fori_loop(0, 8, body, 0)


class Columns:
    def __init__(self, net, source, data, sizes):
        self.net, self.source, self.data = net, source, data
        self.plane = PlaneAll(net, data, sizes)

    def spread(self):
        net = self.net
        w, half = net.y * 2 + net.c, lax.div(net.x, 2)
        self.base, self.w = net.slots(8), w
        self.sent = []
        self.alone = jnp.logical_and(net.y == net.z, net.c == half)
        for o in range(4):
            for i in (0, 1):
                z, x = mod4(net.z + o), mod4(net.x + 2 * i)
                rows = pl.ds(pl.multiple_of(lax.div(x, 2) * 16, 16), 16)
                piece = self.source.at[net.z, net.x, z, rows]
                to = self.data.at[z, x, net.y, pl.ds(pl.multiple_of(net.c * 16, 16), 16)]
                copy = pltpu.make_async_remote_copy(
                    src_ref=piece,
                    dst_ref=to,
                    send_sem=net.send.at[self.base + 2 * o + i],
                    recv_sem=net.recv.at[self.base + w],
                    device_id=net.at(z=z, x=x, y=net.z, c=half),
                    device_id_type=MESH,
                )
                self.sent.append(copy)
                if o or i:
                    copy.start()
                    net.copies.append(copy)
                else:
                    here = (piece, to)
        first, (piece, to) = self.sent[0], here

        @pl.when(self.alone)
        def _():
            to[...] = piece[...]

        @pl.when(jnp.logical_not(self.alone))
        def _():
            first.start()

    def wait_first(self):
        @pl.when(jnp.logical_not(self.alone))
        def _():
            self.sent[0].wait_send()

    def start(self):
        net = self.net
        for w in range(8):
            slot = self.data.at[net.z, net.x, w // 2, pl.ds(16 * (w % 2), 16)]
            copy = net.make(slot, slot, net.at(c=1 - net.c), self.base + w)

            @pl.when(jnp.logical_not(jnp.logical_and(self.alone, self.w == w)))
            def _():
                copy.wait_recv()

        self.plane.start()

    def unpack(self, out):
        data = self.data

        def body(y, _):
            for c in (0, 1):
                for half in (0, 1):
                    parts = [
                        data[z, 2 * i + half, y, 16 * c : 16 * c + 16]
                        for z in range(4)
                        for i in (0, 1)
                    ]
                    at = pl.multiple_of(y * 256 + c * 128, 128)
                    out[pl.ds(at, 128), 256 * half : 256 * half + 256] = jnp.concatenate(
                        parts, axis=0
                    )
            return 0

        lax.fori_loop(0, 4, body, 0)


def share_of(ref, z, x):
    return ref[z, x].reshape(128, 256)


def wide_of(ref, z):
    return jnp.concatenate([share_of(ref, z, x) for x in range(4)], axis=1)


def kernel(
    student_in,
    norm_gain,
    gate_weight,
    up_weight,
    down_weight,
    projection,
    teacher_in,
    teacher_gate,
    teacher_up,
    teacher_down,
    grad_gate,
    grad_up,
    grad_down,
    grad_proj,
    input_grad,
    xin,
    gain,
    wg,
    wu,
    wd,
    pj,
    tin,
    tg,
    tu,
    td,
    tdt,
    parts,
    mate,
    ring,
    thid,
    feat,
    feat1,
    featm,
    feat2,
    sums,
    sums1,
    summ,
    sums2,
    normed,
    summed,
    bgrad,
    ncols,
    scols,
    bcols,
    flat,
    nflat,
    hids,
    errs,
    ggs,
    gate,
    upsum,
    sigma,
    acc,
    acc2,
    tshare,
    target,
    fgrad,
    stat,
    statx,
    statz,
    invs,
    ogg,
    ogu,
    ogd,
    ogp,
    oig,
    load,
    store,
    send,
    recv,
):
    net = Net(send, recv)
    z, x, y, c = net.z, net.x, net.y, net.c
    ys = [mod4(y + o) for o in range(4)]

    loads = {}
    for i, (name, src, dst) in enumerate(
        (
            ("tin", teacher_in, tin),
            ("tg", teacher_gate, tg),
            ("tu", teacher_up, tu),
            ("xin", student_in, xin),
            ("gain", norm_gain, gain),
            ("wg", gate_weight, wg),
            ("wu", up_weight, wu),
            ("wd", down_weight, wd),
            ("td", teacher_down, td),
            ("pj", projection, pj),
        )
    ):
        loads[name] = pltpu.make_async_copy(src, dst, load.at[i])
        loads[name].start()

    barrier = pltpu.get_barrier_semaphore()
    peers = [net.at(y=mod4(y + o), c=lax.rem(c + f, 2)) for o in range(4) for f in (0, 1) if o or f]
    peers += [net.along("x", o) for o in (1, 2, 3)] + [net.along("z", o) for o in (1, 2, 3)]
    for peer in peers:
        pl.semaphore_signal(barrier, inc=1, device_id=peer, device_id_type=MESH)
    near = 2 * c + lax.rem(x, 2)
    for o in range(4):
        for f in (0, 1):
            source = net.at(z=y, x=near, y=mod4(y + o), c=lax.rem(c + f, 2))
            if o or f:
                pl.semaphore_signal(barrier, inc=1, device_id=source, device_id_type=MESH)
            else:

                @pl.when(jnp.logical_or(z != y, x != near))
                def _():
                    pl.semaphore_signal(barrier, inc=1, device_id=source, device_id_type=MESH)

    tsum = RingSum(
        net, "y", lambda d, h: parts.at[d, c, pl.ds(64 * h, 64)], ring
    )
    for name in ("tin", "tg", "tu"):
        loads[name].wait()
    pair = {}

    def project(o):
        d = ys[o]
        rows = tin[pl.ds(pl.multiple_of(d * 256, 256), 256), :]
        parts[d, :, :, 0:896] = mm(rows, tg[...], NN).astype(BF16).reshape(2, 128, 896)
        parts[d, :, :, 896:1792] = mm(rows, tu[...], NN).astype(BF16).reshape(2, 128, 896)

    def swap(o):
        d = ys[o]
        pair[o] = net.put(parts.at[d, 1 - c], mate.at[d], net.at(c=1 - c))

    def join(o):
        d = ys[o]
        pair[o].wait_recv()
        parts[d, c] = (up(parts[d, c]) + up(mate[d])).astype(BF16)

    project(2)
    own = jnp.logical_and(y == z, c == lax.div(x, 2)).astype(jnp.int32)
    pl.semaphore_wait(barrier, len(peers) + 8 - own)
    swap(2)
    project(1)
    swap(1)
    join(2)
    tsum.far()
    project(3)
    swap(3)
    join(1)
    tsum.near_r()

    loads["xin"].wait()
    loads["gain"].wait()

    def squares(b, total):
        v = up(xin[:, pl.ds(pl.multiple_of(b * 256, 256), 256)])
        return total + v * v

    total = lax.fori_loop(0, 16, squares, jnp.zeros((128, 256), F32))
    inv = lax.rsqrt(jnp.sum(total, axis=1, keepdims=True) / 4096.0 + 1e-05)
    invs[...] = jnp.broadcast_to(inv, (128, 128))

    def norm(b, _):
        at = pl.ds(pl.multiple_of(b * 256, 256), 256)
        scale = jnp.concatenate([invs[...], invs[...]], axis=1)
        v = up(xin[:, at]) * scale * gain[:, at]
        normed[lax.div(b, 4), lax.rem(b, 4)] = v.astype(BF16).reshape(4, 32, 256)
        return 0

    lax.fori_loop(0, 16, norm, 0)

    for name in ("wg", "wu", "wd"):
        loads[name].wait()

    def students(first, second, source, out_first, out_second):
        def body(b, _):
            at = pl.ds(pl.multiple_of(b * 1024, 1024), 1024)
            wide = wide_of(source, b)
            out_first[...] += mm(first[:, at], wide, NT)
            if second is not None:
                out_second[...] += mm(second[:, at], wide, NT)
            return 0

        out_first[...] = jnp.zeros(out_first.shape, F32)
        if second is not None:
            out_second[...] = jnp.zeros(out_second.shape, F32)
        lax.fori_loop(0, 4, body, 0)

    def back(out, pairs):
        def body(b, _):
            at = pl.ds(pl.multiple_of(b * 1024, 1024), 1024)
            v = sum(mm(small, w[:, at], TN) for small, w in pairs).astype(BF16)
            for i in range(4):
                out[b, i] = v[:, 256 * i : 256 * i + 256].reshape(4, 32, 256)
            return 0

        lax.fori_loop(0, 4, body, 0)

    def plane_sums(n):
        data = sums.at[n]
        q = (pl.ds(0, 2), pl.ds(2, 2))
        return [
            PlaneSum(
                net,
                ("x", "z"),
                lambda d: data.at[:, d, q[0]],
                sums1.at[n, 0],
                summ.at[n, 0],
                sums2.at[n, 0],
            ),
            PlaneSum(
                net,
                ("z", "x"),
                lambda d: data.at[d, :, q[1]],
                sums1.at[n, 1],
                summ.at[n, 1],
                sums2.at[n, 1],
            ),
        ]

    students(wg, wu, normed, gate, upsum)
    join(3)
    tsum.near_l()
    sig = jax.nn.sigmoid(gate[...])
    sigma[...] = sig
    hid = (gate[...] * sig * upsum[...]).astype(BF16)
    hiddens = TokenDirect(net, hids)
    hiddens.own[...] = hid
    back(sums.at[0], ((hid, wd),))
    branch = plane_sums(0)
    for s in branch:
        s.start()
    tsum.relay()
    project(0)
    swap(0)
    loads["td"].wait()
    tdt[...] = td[...].T
    join(0)
    for s in branch:
        s.turn()

    first, second = tsum.finish()
    sums_all = jnp.concatenate([first, second], axis=0)
    g = sums_all[:, :896]
    teach = g * jax.nn.sigmoid(g) * sums_all[:, 896:]
    teachers = TokenAll(net, thid)
    teachers.own[...] = teach.T.astype(BF16)
    teachers.start()

    order = [ys[0], ys[1], ys[3], ys[2]]

    def group(k):
        d = order[k]
        if k % 2 == 0:
            axes, src = ("x", "z"), lambda e: feat.at[:, e, d]
        else:
            axes, src = ("z", "x"), lambda e: feat.at[e, :, d]
        return PlaneSum(net, axes, src, feat1.at[k], featm.at[k], feat2.at[k])

    teaching = [group(k) for k in range(4)]

    def feature(k, o):
        d = ys[o]
        teachers.wait(o)
        v = mm(tdt[...], thid[:, pl.ds(pl.multiple_of(d * 256, 256), 256)], NN).astype(BF16)
        for f in (0, 1):
            feat[:, :, d, 64 * f : 64 * f + 64] = v[:, 128 * f : 128 * f + 128].reshape(
                4, 4, 64, 128
            )
        teaching[k].start()

    rows_of = lambda j: pl.ds(64 * j, 64)
    share_at = pl.ds(pl.multiple_of((z * 4 + x) * 256, 256), 256)
    for j in (0, 1):
        v = branch[j].finish().reshape(64, 256)
        summed[z, x, 2 * j : 2 * j + 2] = (
            (up(xin[rows_of(j), share_at]) + v).astype(BF16).reshape(2, 32, 256)
        )
    sizes = (sums2.at[0, 0], sums1.at[0, 0])
    sum_all = PlaneAll(net, summed, sizes)
    sum_all.start()
    feature(0, 0)
    teachers.relay()
    sum_all.turn()
    teachers.near()
    feature(1, 1)
    feature(2, 3)
    teachers.finish()
    feature(3, 2)
    teaching[0].turn()
    ncol = Direct(net, normed, ncols)
    ncol.start((2, 0))
    sum_all.finish()
    loads["pj"].wait()
    students(pj, None, summed, acc, None)

    sent = net.group(target.at[pl.ds(0, 448)])

    def hand(k, v):
        d = order[k]
        tshare[d] = v.astype(BF16)
        to = target.at[pl.ds(pl.multiple_of((y * 2 + c) * 64, 64), 64)]
        for f in (0, 1):
            cc = lax.rem(c + f, 2)
            piece = tshare.at[d, pl.ds(pl.multiple_of(cc * 64, 64), 64)]
            if k == 0 and f == 0:
                to[...] = piece[...]
            else:
                sent.put(piece, to, net.at(y=d, c=cc))

    teaching[1].turn()
    hand(0, teaching[0].finish())
    teaching[2].turn()
    hand(1, teaching[1].finish())
    teaching[3].turn()
    hand(2, teaching[2].finish())
    hand(3, teaching[3].finish())
    sent.wait_recv()

    err = ((acc[...] - up(target[...])) * (1.0 / 32.0)).astype(BF16)
    errors = TokenDirect(net, errs)
    errors.own[...] = err
    errors.start()
    back(sums.at[1], ((err, pj),))
    grads = plane_sums(1)
    for s in grads:
        s.start()
    scol = Direct(net, summed, scols)
    scol.start((2, 0))
    for s in grads:
        s.turn()
    for j in (0, 1):
        v = grads[j].finish()
        fgrad[rows_of(j), :] = v.reshape(64, 256)
        bgrad[z, x, 2 * j : 2 * j + 2] = v.astype(BF16)
    grad_all = PlaneAll(net, bgrad, sizes)
    grad_all.start()
    bcol = Columns(net, bgrad, bcols, sizes)
    bcol.spread()
    errors.pass_on()
    scol.start((1, 3))
    hiddens.start()
    grad_all.turn()
    errors.finish()
    bcol.start()
    grad_all.finish()

    students(wd, None, bgrad, acc2, None)
    hg = acc2[...]
    g, s = gate[...], sigma[...]
    gg = (hg * upsum[...] * s * (1.0 + g * (1.0 - s))).astype(BF16)
    ug = (hg * g * s).astype(BF16)
    moment = jnp.sum(up(gg) * g + up(ug) * upsum[...], axis=0, keepdims=True)
    gates = TokenDirect(net, ggs)
    own_at = pl.ds(pl.multiple_of((y * 2 + c) * 128, 128), 128)
    ggs[0:448, own_at] = gg
    ggs[448:896, own_at] = ug
    gates.start()
    ncol.start((1, 3))

    def tell(ref, me, axis):
        group = net.group(ref.at[pl.ds(0, 3)])
        for o in (2, 1, 3):
            group.put(ref.at[me], ref.at[me], net.along(axis, o))
        return group

    statx[x] = jnp.broadcast_to(moment, (8, 128))
    stats = tell(statx, x, "x")
    bcol.plane.turn()
    back(sums.at[2], ((gg, wg), (ug, wu)))
    inner = plane_sums(2)
    for s in inner:
        s.start()
    stats.wait_recv()
    statz[z] = statx[0] + statx[1] + statx[2] + statx[3]
    stats = tell(statz, z, "z")
    hiddens.pass_on()
    scol.unpack(flat)

    outs = []

    def write(i, src, dst):
        outs.append(pltpu.make_async_copy(src, dst, store.at[i]))
        outs[-1].start()

    ogp[...] = mm(errs[...], flat[...], NN).astype(BF16)
    write(0, ogp, grad_proj)
    for s in inner:
        s.turn()
    stats.wait_recv()
    whole = (statz[0] + statz[1] + statz[2] + statz[3]) / 4096.0
    stat[...] = jnp.broadcast_to(whole[0:1], (128, 128)).T
    gates.pass_on()
    for j in (0, 1):
        v = inner[j].finish().reshape(64, 256)
        r = rows_of(j)
        scale = jnp.concatenate([invs[r, :], invs[r, :]], axis=1)
        mean = jnp.concatenate([stat[r, :], stat[r, :]], axis=1)
        scaled = v * gain[:, share_at]
        oig[r, :] = fgrad[r, :] + scale * (scaled - up(xin[r, share_at]) * scale * mean)
    write(1, oig, input_grad)
    gates.finish()
    ncol.unpack(nflat)
    ogg[...] = mm(ggs[0:448], nflat[...], NN).astype(BF16)
    write(2, ogg, grad_gate)
    ogu[...] = mm(ggs[448:896], nflat[...], NN).astype(BF16)
    write(3, ogu, grad_up)
    bcol.plane.finish()
    bcol.unpack(flat)
    hiddens.finish()
    ogd[...] = mm(hids[...], flat[...], NN).astype(BF16)
    write(4, ogd, grad_down)
    bcol.wait_first()
    for copy in net.copies:
        copy.wait_send()
    for copy in outs:
        copy.wait()


def move(*refs):
    srcs, dsts, held = refs[0:5], refs[5:10], refs[10:15]
    came, went = refs[15], refs[16]
    ins = [pltpu.make_async_copy(s, h, came.at[i]) for i, (s, h) in enumerate(zip(srcs, held))]
    outs = [pltpu.make_async_copy(h, d, went.at[i]) for i, (h, d) in enumerate(zip(held, dsts))]
    for copy in ins:
        copy.start()
    for i, copy in zip(ins, outs):
        i.wait()
        copy.start()
    for copy in outs:
        copy.wait()


def shards(
    student_in,
    norm_gain,
    gate_weight,
    up_weight,
    down_weight,
    projection,
    teacher_in,
    teacher_gate,
    teacher_up,
    teacher_down,
):
    vmem = pltpu.VMEM
    anyspec = pl.BlockSpec(memory_space=pl.ANY)
    shapes = (
        jax.ShapeDtypeStruct((448, 512), BF16),
        jax.ShapeDtypeStruct((448, 512), BF16),
        jax.ShapeDtypeStruct((448, 512), BF16),
        jax.ShapeDtypeStruct((512, 512), BF16),
        jax.ShapeDtypeStruct((128, 256), F32),
    )
    made = pl.pallas_call(
        kernel,
        out_shape=shapes,
        in_specs=[anyspec] * 10,
        out_specs=(anyspec,) * 5,
        scratch_shapes=[
            vmem((128, 4096), BF16),
            vmem((1, 4096), F32),
            vmem((448, 4096), BF16),
            vmem((448, 4096), BF16),
            vmem((448, 4096), BF16),
            vmem((512, 4096), BF16),
            vmem((1024, 1024), BF16),
            vmem((1024, 896), BF16),
            vmem((1024, 896), BF16),
            vmem((896, 1024), BF16),
            vmem((1024, 896), BF16),
            vmem((4, 2, 128, 1792), BF16),
            vmem((4, 128, 1792), BF16),
            vmem((6, 64, 1792), BF16),
            vmem((896, 1024), BF16),
            vmem((4, 4, 4, 128, 128), BF16),
            vmem((4, 3, 4, 128, 128), BF16),
            vmem((4, 4, 128, 128), BF16),
            vmem((4, 3, 128, 128), BF16),
            vmem((3, 4, 4, 4, 32, 256), BF16),
            vmem((3, 2, 3, 4, 2, 32, 256), BF16),
            vmem((3, 2, 4, 2, 32, 256), BF16),
            vmem((3, 2, 3, 2, 32, 256), BF16),
            vmem((4, 4, 4, 32, 256), BF16),
            vmem((4, 4, 4, 32, 256), BF16),
            vmem((4, 4, 4, 32, 256), BF16),
            vmem((8, 2, 4, 32, 256), BF16),
            vmem((8, 2, 4, 32, 256), BF16),
            vmem((4, 4, 4, 32, 256), BF16),
            vmem((1024, 512), BF16),
            vmem((1024, 512), BF16),
            vmem((448, 1024), BF16),
            vmem((512, 1024), BF16),
            vmem((896, 1024), BF16),
            vmem((448, 128), F32),
            vmem((448, 128), F32),
            vmem((448, 128), F32),
            vmem((512, 128), F32),
            vmem((448, 128), F32),
            vmem((4, 128, 128), BF16),
            vmem((512, 128), BF16),
            vmem((128, 256), F32),
            vmem((128, 128), F32),
            vmem((4, 8, 128), F32),
            vmem((4, 8, 128), F32),
            vmem((128, 128), F32),
            vmem((448, 512), BF16),
            vmem((448, 512), BF16),
            vmem((448, 512), BF16),
            vmem((512, 512), BF16),
            vmem((128, 256), F32),
            pltpu.SemaphoreType.DMA((10,)),
            pltpu.SemaphoreType.DMA((5,)),
            pltpu.SemaphoreType.DMA((SEMS,)),
            pltpu.SemaphoreType.DMA((SEMS,)),
        ],
        compiler_params=pltpu.CompilerParams(
            collective_id=0, has_side_effects=True, vmem_limit_bytes=67043328
        ),
    )(
        student_in,
        norm_gain.reshape(1, -1),
        gate_weight.T,
        up_weight.T,
        down_weight,
        projection.transpose(1, 2, 0).reshape(512, -1),
        teacher_in,
        teacher_gate,
        teacher_up,
        teacher_down,
    )
    gg, gu, gd, gp, ig = pl.pallas_call(
        move,
        out_shape=shapes,
        in_specs=[anyspec] * 5,
        out_specs=(anyspec,) * 5,
        scratch_shapes=[vmem(s.shape, s.dtype) for s in shapes]
        + [pltpu.SemaphoreType.DMA((5,)), pltpu.SemaphoreType.DMA((5,))],
    )(*made)
    return gg.T, gu.T, gd, gp.reshape(8, 64, 512).transpose(2, 0, 1), ig


def solution(mesh):
    split = Mesh(mesh.devices.reshape(2, 4, 2, 2, 4), ("zh", "y", "c", "zl", "x"))
    in_specs = (
        P(WID, None),
        P(),
        P(None, GH),
        P(None, GH),
        P(GH, None),
        P(None, None, GH),
        P(None, WID),
        P(WID, GH),
        P(WID, GH),
        P(GH, WID),
    )
    out_specs = (
        P(WID, GH),
        P(WID, GH),
        P(GH, WID),
        P(WID, None, GH),
        P(WID, GH),
    )
    return jax.shard_map(
        shards, mesh=split, in_specs=in_specs, out_specs=out_specs, check_vma=False
    )
```

time: 148 us -> 114 us (0.77); the launches traced: 146 us -> 114 us
  Pallas kernels: 138 us -> 113 us
  local copies, waits for them, and re-layouts: 8.01 us -> 0 us
    pallas_call x1 -> x2, Pallas kernels: 138 us -> 113 us  [the longest x1 111 us: shards(): pl.pallas_call(kernel, out_shape=shapes, in_specs=[anyspec] * 10, out_spe...]
    unnamed x7 -> x0, local copies, waits for them, and re-layouts: 8.01 us -> none
where the time goes in v2:
time: 114 us
  Pallas kernels  113 us (99%)
    pallas_call x1, Pallas kernels, shards(): pl.pallas_call(kernel, out_shape=shapes, in_specs=[anyspec] * 10, out_spe...  111 us
    pallas_call x1, Pallas kernels, shards(): pl.pallas_call(move, out_shape=shapes, in_specs=[anyspec] * 5, out_specs=...  2.39 us

profile of v2, /device:TPU:1, one launch (start us, length us, event | category | flops | bytes accessed | tf_op | source)
XLA Modules:
  0.0 114.1 jit_solution(9659696968383589636)
XLA Ops:
  0.6 110.9 %shard_map.137 = (bf16[448,512]{1,0:T(8,128)(2,1)}, bf16[448,512]{1,0:T(8,128)(2,1)}, bf16[448,512]{1,0:T(8,128)(2,1)}, bf16[512,512]{1,0:T(8,128)(2,1)}, f32[128,256]{1,0:T(8,128)}) custom-call(bf16[128,4096]{1,0:T(8,128)(2,1)} %student_in.1, f32[1,4096]{1,0:T(1,128)} %bitcast.14, bf16[448,4096]{1,0:T(8,128)(2,1)} %bitcast.12, bf16[448,4096]{1,0:T(8,128)(2,1)} %bitcast.13, ...), custom_call_target="tpu_custom_call" | custom-call | tf_op jit(solution)/shard_map/pallas_call | solution.py:829
  111.5 2.4 %shard_map.138 = (bf16[448,512]{1,0:T(8,128)(2,1)}, bf16[448,512]{1,0:T(8,128)(2,1)}, bf16[448,512]{1,0:T(8,128)(2,1)}, bf16[512,512]{1,0:T(8,128)(2,1)}, f32[128,256]{1,0:T(8,128)}) custom-call(bf16[448,512]{1,0:T(8,128)(2,1)} %get-tuple-element.15.refs_0_, bf16[448,512]{1,0:T(8,128)(2,1)} %get-tuple-element.16.refs_1_, ...), custom_call_target="tpu_custom_call" | custom-call | tf_op jit(solution)/shard_map/pallas_call | solution.py:906

commit v3 on v2

--- a/solution.py
+++ b/solution.py
@@ -11,7 +11,8 @@
 BF16 = jnp.bfloat16
 WID = ("y", "c")
 GH = ("zh", "zl", "x")
-SEMS = 86
+SEMS = 95
+ORDER = (0, 2, 1, 3)
 
 NN = (((1,), (0,)), ((), ()))
 NT = (((1,), (1,)), ((), ()))
@@ -162,29 +163,29 @@
 
 class PlaneAll:
     def __init__(self, net, data, sizes):
-        self.net, self.data, self.sizes = net, data, sizes
-
-    def copies(self, piece, axis, size):
-        group = self.net.group(size)
+        self.net, self.data, self.sizes, self.groups = net, data, sizes, {}
+
+    def copies(self, q, piece, axis, size):
+        group = self.groups[q] = self.net.group(size)
         for o in (2, 1, 3):
             group.put(piece, piece, self.net.along(axis, o))
-        return group
-
-    def start(self):
-        z, x, size = self.net.z, self.net.x, self.sizes[0]
-        self.a = self.copies(self.data.at[z, x, pl.ds(0, 2)], "z", size)
-        self.b = self.copies(self.data.at[z, x, pl.ds(2, 2)], "x", size)
-
-    def turn(self):
-        z, x, size = self.net.z, self.net.x, self.sizes[1]
-        self.a.wait_recv()
-        self.a = self.copies(self.data.at[:, x, pl.ds(0, 2)], "x", size)
-        self.b.wait_recv()
-        self.b = self.copies(self.data.at[z, :, pl.ds(2, 2)], "z", size)
+
+    def start(self, *blocks):
+        for q in blocks:
+            piece = self.data.at[self.net.z, self.net.x, q]
+            self.copies(q, piece, "z" if q < 2 else "x", self.sizes[0])
+
+    def turn(self, *blocks):
+        for q in blocks:
+            self.groups[q].wait_recv()
+            if q < 2:
+                self.copies(q, self.data.at[:, self.net.x, q], "x", self.sizes[1])
+            else:
+                self.copies(q, self.data.at[self.net.z, :, q], "z", self.sizes[1])
 
     def finish(self):
-        self.a.wait_recv()
-        self.b.wait_recv()
+        for q in ORDER:
+            self.groups[q].wait_recv()
 
 
 class TokenDirect:
@@ -199,18 +200,20 @@
     def start(self):
         net, own = self.net, self.own
         self.mate = net.at(c=1 - net.c)
-        self.far = [(4 - o, net.put(own, own, net.along("y", o))) for o in (2, 1, 3)]
-        self.near = [net.put(own, own, self.mate)]
+        self.far = net.group(self.data.at[:, pl.ds(0, 384)])
+        self.near = net.group(self.data.at[:, pl.ds(0, 512)])
+        for o in (2, 1, 3):
+            self.far.put(own, own, net.along("y", o))
+        self.near.put(own, own, self.mate)
 
     def pass_on(self):
-        for o, copy in self.far:
-            copy.wait_recv()
+        self.far.wait_recv()
+        for o in (2, 1, 3):
             piece = self.slot(o)
-            self.near.append(self.net.put(piece, piece, self.mate))
+            self.near.put(piece, piece, self.mate)
 
     def finish(self):
-        for copy in self.near:
-            copy.wait_recv()
+        self.near.wait_recv()
 
 
 class TokenAll:
@@ -347,7 +350,7 @@
             def _():
                 copy.wait_recv()
 
-        self.plane.start()
+        self.plane.start(*ORDER)
 
     def unpack(self, out):
         data = self.data
@@ -453,12 +456,16 @@
     z, x, y, c = net.z, net.x, net.y, net.c
     ys = [mod4(y + o) for o in range(4)]
 
+    rows_in = [pl.ds(pl.multiple_of(d * 256, 256), 256) for d in ys]
     loads = {}
     for i, (name, src, dst) in enumerate(
         (
-            ("tin", teacher_in, tin),
+            (2, teacher_in.at[rows_in[2]], tin.at[rows_in[2]]),
             ("tg", teacher_gate, tg),
             ("tu", teacher_up, tu),
+            (1, teacher_in.at[rows_in[1]], tin.at[rows_in[1]]),
+            (3, teacher_in.at[rows_in[3]], tin.at[rows_in[3]]),
+            (0, teacher_in.at[rows_in[0]], tin.at[rows_in[0]]),
             ("xin", student_in, xin),
             ("gain", norm_gain, gain),
             ("wg", gate_weight, wg),
@@ -491,14 +498,17 @@
     tsum = RingSum(
         net, "y", lambda d, h: parts.at[d, c, pl.ds(64 * h, 64)], ring
     )
-    for name in ("tin", "tg", "tu"):
-        loads[name].wait()
     pair = {}
 
     def project(o):
         d = ys[o]
-        rows = tin[pl.ds(pl.multiple_of(d * 256, 256), 256), :]
+        loads[o].wait()
+        rows = tin[rows_in[o], :]
+        if o == 2:
+            loads["tg"].wait()
         parts[d, :, :, 0:896] = mm(rows, tg[...], NN).astype(BF16).reshape(2, 128, 896)
+        if o == 2:
+            loads["tu"].wait()
         parts[d, :, :, 896:1792] = mm(rows, tu[...], NN).astype(BF16).reshape(2, 128, 896)
 
     def swap(o):
@@ -572,25 +582,15 @@
 
     def plane_sums(n):
         data = sums.at[n]
-        q = (pl.ds(0, 2), pl.ds(2, 2))
-        return [
-            PlaneSum(
-                net,
-                ("x", "z"),
-                lambda d: data.at[:, d, q[0]],
-                sums1.at[n, 0],
-                summ.at[n, 0],
-                sums2.at[n, 0],
-            ),
-            PlaneSum(
-                net,
-                ("z", "x"),
-                lambda d: data.at[d, :, q[1]],
-                sums1.at[n, 1],
-                summ.at[n, 1],
-                sums2.at[n, 1],
-            ),
-        ]
+
+        def block(q):
+            if q < 2:
+                axes, src = ("x", "z"), lambda d: data.at[:, d, q]
+            else:
+                axes, src = ("z", "x"), lambda d: data.at[d, :, q]
+            return PlaneSum(net, axes, src, sums1.at[n, q], summ.at[n, q], sums2.at[n, q])
+
+        return [block(q) for q in range(4)]
 
     students(wg, wu, normed, gate, upsum)
     join(3)
@@ -602,16 +602,16 @@
     hiddens.own[...] = hid
     back(sums.at[0], ((hid, wd),))
     branch = plane_sums(0)
-    for s in branch:
-        s.start()
+    for q in ORDER:
+        branch[q].start()
     tsum.relay()
     project(0)
     swap(0)
     loads["td"].wait()
     tdt[...] = td[...].T
     join(0)
-    for s in branch:
-        s.turn()
+    for q in ORDER:
+        branch[q].turn()
 
     first, second = tsum.finish()
     sums_all = jnp.concatenate([first, second], axis=0)
@@ -643,27 +643,25 @@
             )
         teaching[k].start()
 
-    rows_of = lambda j: pl.ds(64 * j, 64)
+    rows_of = lambda q: pl.ds(32 * q, 32)
     share_at = pl.ds(pl.multiple_of((z * 4 + x) * 256, 256), 256)
-    for j in (0, 1):
-        v = branch[j].finish().reshape(64, 256)
-        summed[z, x, 2 * j : 2 * j + 2] = (
-            (up(xin[rows_of(j), share_at]) + v).astype(BF16).reshape(2, 32, 256)
-        )
     sizes = (sums2.at[0, 0], sums1.at[0, 0])
     sum_all = PlaneAll(net, summed, sizes)
-    sum_all.start()
+    for q in ORDER:
+        v = branch[q].finish()
+        summed[z, x, q] = (up(xin[rows_of(q), share_at]) + v).astype(BF16)
+        sum_all.start(q)
     feature(0, 0)
     teachers.relay()
-    sum_all.turn()
+    sum_all.turn(*ORDER)
     teachers.near()
     feature(1, 1)
     feature(2, 3)
+    teaching[0].turn()
     teachers.finish()
     feature(3, 2)
-    teaching[0].turn()
     ncol = Direct(net, normed, ncols)
-    ncol.start((2, 0))
+    ncol.start((2, 1, 3, 0))
     sum_all.finish()
     loads["pj"].wait()
     students(pj, None, summed, acc, None)
@@ -683,12 +681,10 @@
                 sent.put(piece, to, net.at(y=d, c=cc))
 
     teaching[1].turn()
-    hand(0, teaching[0].finish())
     teaching[2].turn()
-    hand(1, teaching[1].finish())
     teaching[3].turn()
-    hand(2, teaching[2].finish())
-    hand(3, teaching[3].finish())
+    for k in range(4):
+        hand(k, teaching[k].finish())
     sent.wait_recv()
 
     err = ((acc[...] - up(target[...])) * (1.0 / 32.0)).astype(BF16)
@@ -697,24 +693,25 @@
     errors.start()
     back(sums.at[1], ((err, pj),))
     grads = plane_sums(1)
-    for s in grads:
-        s.start()
+    for q in ORDER:
+        grads[q].start()
     scol = Direct(net, summed, scols)
     scol.start((2, 0))
-    for s in grads:
-        s.turn()
-    for j in (0, 1):
-        v = grads[j].finish()
-        fgrad[rows_of(j), :] = v.reshape(64, 256)
-        bgrad[z, x, 2 * j : 2 * j + 2] = v.astype(BF16)
+    for q in ORDER:
+        grads[q].turn()
     grad_all = PlaneAll(net, bgrad, sizes)
-    grad_all.start()
+    for q in ORDER:
+        v = grads[q].finish()
+        bgrad[z, x, q] = v.astype(BF16)
+        grad_all.start(q)
+        fgrad[rows_of(q), :] = v
     bcol = Columns(net, bgrad, bcols, sizes)
     bcol.spread()
+    grad_all.turn(0, 2)
     errors.pass_on()
     scol.start((1, 3))
     hiddens.start()
-    grad_all.turn()
+    grad_all.turn(1, 3)
     errors.finish()
     bcol.start()
     grad_all.finish()
@@ -730,7 +727,6 @@
     ggs[0:448, own_at] = gg
     ggs[448:896, own_at] = ug
     gates.start()
-    ncol.start((1, 3))
 
     def tell(ref, me, axis):
         group = net.group(ref.at[pl.ds(0, 3)])
@@ -740,11 +736,12 @@
 
     statx[x] = jnp.broadcast_to(moment, (8, 128))
     stats = tell(statx, x, "x")
-    bcol.plane.turn()
+    bcol.plane.turn(0, 2)
     back(sums.at[2], ((gg, wg), (ug, wu)))
     inner = plane_sums(2)
-    for s in inner:
-        s.start()
+    for q in ORDER:
+        inner[q].start()
+    bcol.plane.turn(1, 3)
     stats.wait_recv()
     statz[z] = statx[0] + statx[1] + statx[2] + statx[3]
     stats = tell(statz, z, "z")
@@ -759,22 +756,11 @@
 
     ogp[...] = mm(errs[...], flat[...], NN).astype(BF16)
     write(0, ogp, grad_proj)
-    for s in inner:
-        s.turn()
-    stats.wait_recv()
-    whole = (statz[0] + statz[1] + statz[2] + statz[3]) / 4096.0
-    stat[...] = jnp.broadcast_to(whole[0:1], (128, 128)).T
+    ncol.unpack(nflat)
+    for q in ORDER:
+        inner[q].turn()
     gates.pass_on()
-    for j in (0, 1):
-        v = inner[j].finish().reshape(64, 256)
-        r = rows_of(j)
-        scale = jnp.concatenate([invs[r, :], invs[r, :]], axis=1)
-        mean = jnp.concatenate([stat[r, :], stat[r, :]], axis=1)
-        scaled = v * gain[:, share_at]
-        oig[r, :] = fgrad[r, :] + scale * (scaled - up(xin[r, share_at]) * scale * mean)
-    write(1, oig, input_grad)
     gates.finish()
-    ncol.unpack(nflat)
     ogg[...] = mm(ggs[0:448], nflat[...], NN).astype(BF16)
     write(2, ogg, grad_gate)
     ogu[...] = mm(ggs[448:896], nflat[...], NN).astype(BF16)
@@ -784,6 +770,17 @@
     hiddens.finish()
     ogd[...] = mm(hids[...], flat[...], NN).astype(BF16)
     write(4, ogd, grad_down)
+    stats.wait_recv()
+    whole = (statz[0] + statz[1] + statz[2] + statz[3]) / 4096.0
+    stat[...] = jnp.broadcast_to(whole[0:1], (128, 128)).T
+    for q in ORDER:
+        v = inner[q].finish()
+        r = rows_of(q)
+        scale = jnp.concatenate([invs[r, :], invs[r, :]], axis=1)
+        mean = jnp.concatenate([stat[r, :], stat[r, :]], axis=1)
+        scaled = v * gain[:, share_at]
+        oig[r, :] = fgrad[r, :] + scale * (scaled - up(xin[r, share_at]) * scale * mean)
+    write(1, oig, input_grad)
     bcol.wait_first()
     for copy in net.copies:
         copy.wait_send()
@@ -852,9 +849,9 @@
             vmem((4, 4, 128, 128), BF16),
             vmem((4, 3, 128, 128), BF16),
             vmem((3, 4, 4, 4, 32, 256), BF16),
-            vmem((3, 2, 3, 4, 2, 32, 256), BF16),
-            vmem((3, 2, 4, 2, 32, 256), BF16),
-            vmem((3, 2, 3, 2, 32, 256), BF16),
+            vmem((3, 4, 3, 4, 32, 256), BF16),
+            vmem((3, 4, 4, 32, 256), BF16),
+            vmem((3, 4, 3, 32, 256), BF16),
             vmem((4, 4, 4, 32, 256), BF16),
             vmem((4, 4, 4, 32, 256), BF16),
             vmem((4, 4, 4, 32, 256), BF16),
@@ -883,7 +880,7 @@
             vmem((448, 512), BF16),
             vmem((512, 512), BF16),
             vmem((128, 256), F32),
-            pltpu.SemaphoreType.DMA((10,)),
+            pltpu.SemaphoreType.DMA((13,)),
             pltpu.SemaphoreType.DMA((5,)),
             pltpu.SemaphoreType.DMA((SEMS,)),
             pltpu.SemaphoreType.DMA((SEMS,)),

time: 114 us -> 109 us (0.956)
  Pallas kernels: 113 us -> 108 us
    pallas_call x1, Pallas kernels: 111 us -> 106 us  [shards(): pl.pallas_call(kernel, out_shape=shapes, in_specs=[anyspec] * 10, out_spe...]
where the time goes in v3:
time: 109 us
  Pallas kernels  108 us (99%)
    pallas_call x1, Pallas kernels, shards(): pl.pallas_call(kernel, out_shape=shapes, in_specs=[anyspec] * 10, out_spe...  106 us
    pallas_call x1, Pallas kernels, shards(): pl.pallas_call(move, out_shape=shapes, in_specs=[anyspec] * 5, out_specs=...  2.39 us

profile of v3, /device:TPU:1, one launch (start us, length us, event | category | flops | bytes accessed | tf_op | source)
XLA Modules:
  0.0 109.2 jit_solution(1700201643387447954)
XLA Ops:
  0.6 106.0 %shard_map.137 = (bf16[448,512]{1,0:T(8,128)(2,1)}, bf16[448,512]{1,0:T(8,128)(2,1)}, bf16[448,512]{1,0:T(8,128)(2,1)}, bf16[512,512]{1,0:T(8,128)(2,1)}, f32[128,256]{1,0:T(8,128)}) custom-call(bf16[128,4096]{1,0:T(8,128)(2,1)} %student_in.1, f32[1,4096]{1,0:T(1,128)} %bitcast.14, bf16[448,4096]{1,0:T(8,128)(2,1)} %bitcast.12, bf16[448,4096]{1,0:T(8,128)(2,1)} %bitcast.13, ...), custom_call_target="tpu_custom_call" | custom-call | tf_op jit(solution)/shard_map/pallas_call | solution.py:826
  106.7 2.4 %shard_map.138 = (bf16[448,512]{1,0:T(8,128)(2,1)}, bf16[448,512]{1,0:T(8,128)(2,1)}, bf16[448,512]{1,0:T(8,128)(2,1)}, bf16[512,512]{1,0:T(8,128)(2,1)}, f32[128,256]{1,0:T(8,128)}) custom-call(bf16[448,512]{1,0:T(8,128)(2,1)} %get-tuple-element.15.refs_0_, bf16[448,512]{1,0:T(8,128)(2,1)} %get-tuple-element.16.refs_1_, ...), custom_call_target="tpu_custom_call" | custom-call | tf_op jit(solution)/shard_map/pallas_call | solution.py:903

commit v4 on v3

--- a/solution.py
+++ b/solution.py
@@ -11,7 +11,7 @@
 BF16 = jnp.bfloat16
 WID = ("y", "c")
 GH = ("zh", "zl", "x")
-SEMS = 95
+SEMS = 101
 ORDER = (0, 2, 1, 3)
 
 NN = (((1,), (0,)), ((), ()))
@@ -186,6 +186,34 @@
     def finish(self):
         for q in ORDER:
             self.groups[q].wait_recv()
+
+    def ring_parts(self):
+        net, data = self.net, self.data
+        return (
+            ("x", lambda d: data.at[:, d, pl.ds(0, 2)], lambda d, h: data.at[:, d, h]),
+            ("z", lambda d: data.at[d, :, pl.ds(2, 2)], lambda d, h: data.at[d, :, 2 + h]),
+        )
+
+    def ring_turn(self):
+        net, self.near = self.net, []
+        for i, (axis, whole, _) in enumerate(self.ring_parts()):
+            for q in (2 * i, 2 * i + 1):
+                self.groups[q].wait_recv()
+            own = whole(getattr(net, axis))
+            self.near += [net.put(own, own, net.along(axis, o)) for o in (1, 3)]
+
+    def ring_relay(self):
+        net, self.far = self.net, []
+        for i, (axis, _, part) in enumerate(self.ring_parts()):
+            me = getattr(net, axis)
+            for j, (o, h) in enumerate(((1, 0), (3, 1))):
+                self.near[2 * i + j].wait_recv()
+                piece = part(mod4(me + 4 - o), h)
+                self.far.append(net.put(piece, piece, net.along(axis, o)))
+
+    def ring_finish(self):
+        for copy in self.far:
+            copy.wait_recv()
 
 
 class TokenDirect:
@@ -653,19 +681,16 @@
         sum_all.start(q)
     feature(0, 0)
     teachers.relay()
-    sum_all.turn(*ORDER)
+    sum_all.ring_turn()
     teachers.near()
     feature(1, 1)
+    teachers.finish()
     feature(2, 3)
     teaching[0].turn()
-    teachers.finish()
     feature(3, 2)
+    sum_all.ring_relay()
     ncol = Direct(net, normed, ncols)
     ncol.start((2, 1, 3, 0))
-    sum_all.finish()
-    loads["pj"].wait()
-    students(pj, None, summed, acc, None)
-
     sent = net.group(target.at[pl.ds(0, 448)])
 
     def hand(k, v):
@@ -683,6 +708,9 @@
     teaching[1].turn()
     teaching[2].turn()
     teaching[3].turn()
+    sum_all.ring_finish()
+    loads["pj"].wait()
+    students(pj, None, summed, acc, None)
     for k in range(4):
         hand(k, teaching[k].finish())
     sent.wait_recv()
@@ -722,11 +750,12 @@
     gg = (hg * upsum[...] * s * (1.0 + g * (1.0 - s))).astype(BF16)
     ug = (hg * g * s).astype(BF16)
     moment = jnp.sum(up(gg) * g + up(ug) * upsum[...], axis=0, keepdims=True)
-    gates = TokenDirect(net, ggs)
+    gates = [TokenDirect(net, ggs.at[pl.ds(448 * i, 448)]) for i in (0, 1)]
     own_at = pl.ds(pl.multiple_of((y * 2 + c) * 128, 128), 128)
     ggs[0:448, own_at] = gg
     ggs[448:896, own_at] = ug
-    gates.start()
+    gates[0].start()
+    gates[1].start()
 
     def tell(ref, me, axis):
         group = net.group(ref.at[pl.ds(0, 3)])
@@ -757,12 +786,14 @@
     ogp[...] = mm(errs[...], flat[...], NN).astype(BF16)
     write(0, ogp, grad_proj)
     ncol.unpack(nflat)
+    gates[0].pass_on()
     for q in ORDER:
         inner[q].turn()
-    gates.pass_on()
-    gates.finish()
+    gates[0].finish()
     ogg[...] = mm(ggs[0:448], nflat[...], NN).astype(BF16)
     write(2, ogg, grad_gate)
+    gates[1].pass_on()
+    gates[1].finish()
     ogu[...] = mm(ggs[448:896], nflat[...], NN).astype(BF16)
     write(3, ogu, grad_up)
     bcol.plane.finish()

time: 109 us -> 109 us (level)
  no operation moved by 1% of the time
where the time goes in v4:
time: 109 us; the launch traced here: 108 us
  Pallas kernels  108 us (99%)
    pallas_call x1, Pallas kernels, shards(): pl.pallas_call(kernel, out_shape=shapes, in_specs=[anyspec] * 10, out_spe...  105 us
    pallas_call x1, Pallas kernels, shards(): pl.pallas_call(move, out_shape=shapes, in_specs=[anyspec] * 5, out_specs=...  2.39 us

profile of v4, /device:TPU:1, one launch (start us, length us, event | category | flops | bytes accessed | tf_op | source)
XLA Modules:
  0.0 108.4 jit_solution(15648600755452830942)
XLA Ops:
  0.6 105.2 %shard_map.137 = (bf16[448,512]{1,0:T(8,128)(2,1)}, bf16[448,512]{1,0:T(8,128)(2,1)}, bf16[448,512]{1,0:T(8,128)(2,1)}, bf16[512,512]{1,0:T(8,128)(2,1)}, f32[128,256]{1,0:T(8,128)}) custom-call(bf16[128,4096]{1,0:T(8,128)(2,1)} %student_in.1, f32[1,4096]{1,0:T(1,128)} %bitcast.14, bf16[448,4096]{1,0:T(8,128)(2,1)} %bitcast.12, bf16[448,4096]{1,0:T(8,128)(2,1)} %bitcast.13, ...), custom_call_target="tpu_custom_call" | custom-call | tf_op jit(solution)/shard_map/pallas_call | solution.py:857
  105.8 2.4 %shard_map.138 = (bf16[448,512]{1,0:T(8,128)(2,1)}, bf16[448,512]{1,0:T(8,128)(2,1)}, bf16[448,512]{1,0:T(8,128)(2,1)}, bf16[512,512]{1,0:T(8,128)(2,1)}, f32[128,256]{1,0:T(8,128)}) custom-call(bf16[448,512]{1,0:T(8,128)(2,1)} %get-tuple-element.15.refs_0_, bf16[448,512]{1,0:T(8,128)(2,1)} %get-tuple-element.16.refs_1_, ...), custom_call_target="tpu_custom_call" | custom-call | tf_op jit(solution)/shard_map/pallas_call | solution.py:934

commit v5 on v4

--- a/solution.py
+++ b/solution.py
@@ -822,8 +822,13 @@
 def move(*refs):
     srcs, dsts, held = refs[0:5], refs[5:10], refs[10:15]
     came, went = refs[15], refs[16]
-    ins = [pltpu.make_async_copy(s, h, came.at[i]) for i, (s, h) in enumerate(zip(srcs, held))]
-    outs = [pltpu.make_async_copy(h, d, went.at[i]) for i, (h, d) in enumerate(zip(held, dsts))]
+    ins, outs = [], []
+    for part in range(4):
+        for s, h, d in zip(srcs, held, dsts):
+            rows = pl.ds(part * (s.shape[0] // 4), s.shape[0] // 4)
+            i = len(ins)
+            ins.append(pltpu.make_async_copy(s.at[rows], h.at[rows], came.at[i]))
+            outs.append(pltpu.make_async_copy(h.at[rows], d.at[rows], went.at[i]))
     for copy in ins:
         copy.start()
     for i, copy in zip(ins, outs):
@@ -937,7 +942,7 @@
         in_specs=[anyspec] * 5,
         out_specs=(anyspec,) * 5,
         scratch_shapes=[vmem(s.shape, s.dtype) for s in shapes]
-        + [pltpu.SemaphoreType.DMA((5,)), pltpu.SemaphoreType.DMA((5,))],
+        + [pltpu.SemaphoreType.DMA((20,)), pltpu.SemaphoreType.DMA((20,))],
     )(*made)
     return gg.T, gu.T, gd, gp.reshape(8, 64, 512).transpose(2, 0, 1), ig
 

time: 109 us -> 109 us (level)
  no operation moved by 1% of the time
where the time goes in v5:
time: 109 us
  Pallas kernels  108 us (99%)
    pallas_call x1, Pallas kernels, shards(): pl.pallas_call(kernel, out_shape=shapes, in_specs=[anyspec] * 10, out_spe...  105 us
    pallas_call x1, Pallas kernels, shards(): pl.pallas_call(move, out_shape=shapes, in_specs=[anyspec] * 5, out_specs=...  2.62 us

profile of v5, /device:TPU:1, one launch (start us, length us, event | category | flops | bytes accessed | tf_op | source)
XLA Modules:
  0.0 108.6 jit_solution(2071793422639258801)
XLA Ops:
  0.6 105.2 %shard_map.137 = (bf16[448,512]{1,0:T(8,128)(2,1)}, bf16[448,512]{1,0:T(8,128)(2,1)}, bf16[448,512]{1,0:T(8,128)(2,1)}, bf16[512,512]{1,0:T(8,128)(2,1)}, f32[128,256]{1,0:T(8,128)}) custom-call(bf16[128,4096]{1,0:T(8,128)(2,1)} %student_in.1, f32[1,4096]{1,0:T(1,128)} %bitcast.14, bf16[448,4096]{1,0:T(8,128)(2,1)} %bitcast.12, bf16[448,4096]{1,0:T(8,128)(2,1)} %bitcast.13, ...), custom_call_target="tpu_custom_call" | custom-call | tf_op jit(solution)/shard_map/pallas_call | solution.py:862
  105.8 2.6 %shard_map.138 = (bf16[448,512]{1,0:T(8,128)(2,1)}, bf16[448,512]{1,0:T(8,128)(2,1)}, bf16[448,512]{1,0:T(8,128)(2,1)}, bf16[512,512]{1,0:T(8,128)(2,1)}, f32[128,256]{1,0:T(8,128)}) custom-call(bf16[448,512]{1,0:T(8,128)(2,1)} %get-tuple-element.15.refs_0_, bf16[448,512]{1,0:T(8,128)(2,1)} %get-tuple-element.16.refs_1_, ...), custom_call_target="tpu_custom_call" | custom-call | tf_op jit(solution)/shard_map/pallas_call | solution.py:939
